TPU v7x, 128 devices: a whole 4x4x4 slice. The times are simulated.
128 devices in a mesh: dom: 16 (over x, y_lo, core), cls: 8 (over y_hi, z).
Axes of the slice: x: 4, y: 4 (y_hi: 2, y_lo: 2; y = y_hi * 2 + y_lo), z: 4, core: 2. Of those that a mesh axis runs over, the one named last changes fastest.
Arguments:
- particles: bfloat16 [256, 16640], P('dom'), may hold values from -5 to 5
- references: bfloat16 [16, 16, 16640], P('dom', 'cls'), may hold values from -0.15504342 to 0.15504342
- inv_noise: float32 [8320], replicated, may hold values from 0.3 to 3
- shifts: int32 [128, 2], replicated, may hold values from -5 to 5, as said below
- prior_class: int32 [256], P('dom'), may hold values from 0 to 15
- prior_orient: int32 [256], P('dom'), may hold values from 0 to 15
Outputs:
- back_projection: float32 [16, 16, 16640], P('dom', 'cls')
- class_weights: float32 [16, 16], P('dom', 'cls')
- log_norm: float32 [256], P('dom')
Inputs may be any that keep to these rules, and one draw needn't show every extreme that they name: `shifts`: row 0 is the zero translation and row 1 is (5, -5).
All inputs are finite; a program needn't handle non-finite values.
Results may differ from a plain program's by a relative error of at most 0.0022.
Values may be sent and summed in bfloat16 or wider, within the bound.
A program may use at most 64 MiB of HBM per device.

v0:
```python
import math

import jax
import jax.numpy as jnp
from jax import lax
from jax.sharding import PartitionSpec as P

L = 128


PRIOR_LOG_BOOST = 12.0


def from_root(block, axis, owner):
    block = jnp.where(lax.axis_index(axis) == owner, block, jnp.zeros_like(block))
    return lax.psum(block, axis)


def combined_all(part, axis, combine):
    gathered = jax.tree.map(lambda a: lax.all_gather(a, axis), part)

    def take(source):
        return jax.tree.map(lambda a: lax.dynamic_index_in_dim(a, source, 0, False), gathered)

    return lax.fori_loop(
        1, lax.axis_size(axis), lambda source, state: combine(state, take(source)), take(0)
    )


def phase_table(shifts):
    half_width = L // 2 + 1
    row_index = jnp.arange(L, dtype=jnp.int32)
    freq_y = jnp.where(row_index < L // 2, row_index, row_index - L)
    freq_y = jnp.repeat(freq_y, half_width)
    freq_x = jnp.tile(jnp.arange(half_width, dtype=jnp.int32), L)
    phase_turns = (freq_x[:, None] * shifts[None, :, 0] + freq_y[:, None] * shifts[None, :, 1]) % L
    shift_phase_radians = phase_turns.astype(jnp.float32) * (2.0 * math.pi / L)
    return jnp.concatenate([jnp.cos(shift_phase_radians), jnp.sin(shift_phase_radians)], 0).astype(
        jnp.bfloat16
    )


def correlate(reference_block, parts_real, parts_imag, inv_noise, table):
    width = parts_real.shape[1]
    ref_real = reference_block[:, :width].astype(jnp.float32)
    ref_imag = reference_block[:, width:].astype(jnp.float32)
    prod_real = inv_noise * (
        parts_real[:, None, :] * ref_real[None] + parts_imag[:, None, :] * ref_imag[None]
    )
    prod_imag = inv_noise * (
        parts_imag[:, None, :] * ref_real[None] - parts_real[:, None, :] * ref_imag[None]
    )
    products = jnp.concatenate([prod_real, prod_imag], -1).astype(jnp.bfloat16)
    row_count = parts_real.shape[0]
    orient_count = reference_block.shape[0]
    score_grid = jnp.dot(
        products.reshape(row_count * orient_count, 2 * width),
        table,
        preferred_element_type=jnp.float32,
    )
    score_grid = score_grid.reshape(row_count, orient_count, table.shape[1])
    power = 0.5 * jnp.sum(inv_noise * (ref_real * ref_real + ref_imag * ref_imag), -1)
    return score_grid - power[None, :, None]


def project_back(posterior_floor, parts_real, parts_imag, table):
    width = parts_real.shape[1]
    row_count, orient_count, trans_count = posterior_floor.shape
    coeff = jnp.dot(
        posterior_floor.reshape(row_count * orient_count, trans_count),
        table.T,
        preferred_element_type=jnp.float32,
    )
    coeff = coeff.reshape(row_count, orient_count, 2 * width)
    cos_sum = coeff[:, :, :width]
    sin_sum = coeff[:, :, width:]
    real_part = jnp.sum(parts_real[:, None, :] * cos_sum + parts_imag[:, None, :] * sin_sum, 0)
    imag_part = jnp.sum(parts_imag[:, None, :] * cos_sum - parts_real[:, None, :] * sin_sum, 0)
    return jnp.concatenate([real_part, imag_part], -1)


def lse_combine(first, second):
    top = jnp.maximum(first[0], second[0])
    return (top, first[1] * jnp.exp(first[0] - top) + second[1] * jnp.exp(second[0] - top))


def on_device(particles, references, inv_noise, shifts, prior_class, prior_orient):
    table = phase_table(shifts)
    width = inv_noise.shape[0]
    parts_real = particles[:, :width].astype(jnp.float32)
    parts_imag = particles[:, width:].astype(jnp.float32)
    slots = references.shape[0]
    orient_count = references.shape[1]
    part_count = particles.shape[0]
    trans_count = table.shape[1]
    domain_groups = lax.axis_size("dom")
    classes = slots * domain_groups
    orient_ids = lax.axis_index("cls") * orient_count + jnp.arange(orient_count, dtype=jnp.int32)
    orient_hit = prior_orient[:, None] == orient_ids[None, :]

    def score_class(class_id, carry):
        stored, run_top, run_total = carry
        mine = lax.dynamic_index_in_dim(references, class_id % slots, 0, keepdims=False)
        refs_class = from_root(mine, "dom", class_id // slots)
        score_grid = correlate(refs_class, parts_real, parts_imag, inv_noise, table)
        best_match = orient_hit & (prior_class[:, None] == class_id)
        score_grid = (
            score_grid + jnp.where(best_match, PRIOR_LOG_BOOST, 0.0).astype(jnp.float32)[:, :, None]
        )
        stored = lax.dynamic_update_index_in_dim(stored, score_grid, class_id, 0)
        local_top = jnp.max(score_grid, axis=(1, 2))
        local_total = jnp.sum(jnp.exp(score_grid - local_top[:, None, None]), axis=(1, 2))
        class_top, class_total = combined_all((local_top, local_total), "cls", lse_combine)
        run_top, run_total = lse_combine((run_top, run_total), (class_top, class_total))
        return (stored, run_top, run_total)

    start_carry = (
        jnp.zeros((classes, part_count, orient_count, trans_count), jnp.float32),
        jnp.full((part_count,), -1e30, jnp.float32),
        jnp.zeros((part_count,), jnp.float32),
    )
    stored, run_top, run_total = lax.fori_loop(0, classes, score_class, start_carry)
    top, total = (run_top, run_total)
    log_norm = top + jnp.log(total)

    def back_class(class_id):
        posterior = jnp.exp(stored[class_id] - log_norm[:, None, None])
        weight = jnp.sum(posterior, axis=(0, 2))
        sums = project_back(posterior.astype(jnp.bfloat16), parts_real, parts_imag, table)
        return (sums, weight)

    sums_all, weight_all = lax.map(back_class, jnp.arange(classes, dtype=jnp.int32))
    back_projection, class_weights = (
        lax.psum_scatter(sums_all, "dom", scatter_dimension=0, tiled=True),
        lax.psum_scatter(weight_all, "dom", scatter_dimension=0, tiled=True),
    )
    return (back_projection, class_weights, log_norm)


def solution(mesh):
    placed = (P("dom", None), P("dom", "cls", None), P(), P(), P("dom"), P("dom"))
    return jax.shard_map(
        on_device,
        mesh=mesh,
        in_specs=placed,
        out_specs=(P("dom", "cls", None), P("dom", "cls"), P("dom")),
        check_vma=False,
    )
```

profile of v0, /device:TPU:1, one launch (start us, length us, event | category | flops | bytes accessed | tf_op | source)
XLA Modules:
  0.0 2455.8 jit_solution(5740838051703521263)
XLA Ops:
  10.5 18.1 cosine_convert_fusion
  28.6 17.1 pad_maximum_fusion
  45.7 2152.6 %while.91 = (s32[]{:T(128)}, f32[16,16,2,128]{3,1,2,0:T(8,128)S(1)}, f32[16]{0:T(128)S(1)}, f32[16]{0:T(128)S(1)}, f32[8320]{0:T(1024)S(1)}, /*index=5*/f32[16,8...) while((s32[]{:T(128)}, ...), condition=%wide.region_7.8_spmd.clone, body=%wide.region_0.7_spmd.clone.sunk | while | flops 141344560 | bytes 8527440 | solution.py:122
  47.9 110.5 %all-reduce.14.cloned.1.call-done = bf16[2,16640]{1,0:T(2,128)(2,1)} async-done(((bf16[2,16640]{1,0:T(2,128)(2,1)}), bf16[2,16640]{1,0:T(2,128)(2,1)}) %all-reduce.14.cloned.1.call-update) | async-done | bytes 66576 | tf_op jit(solution)/shard_map/while/body/eval_jaxpr/psum | solution.py:16
  164.4 20.5 all-reduce.8
  187.5 105.3 %all-reduce.14.cloned.1.call-done = bf16[2,16640]{1,0:T(2,128)(2,1)} async-done(((bf16[2,16640]{1,0:T(2,128)(2,1)}), bf16[2,16640]{1,0:T(2,128)(2,1)}) %all-reduce.14.cloned.1.call-update) | async-done | bytes 66576 | tf_op jit(solution)/shard_map/while/body/eval_jaxpr/psum | solution.py:16
  294.9 3.0 bitcast_dynamic-update-slice_fusion.2
  298.8 20.5 all-reduce.8
  321.9 105.3 %all-reduce.14.cloned.1.call-done = bf16[2,16640]{1,0:T(2,128)(2,1)} async-done(((bf16[2,16640]{1,0:T(2,128)(2,1)}), bf16[2,16640]{1,0:T(2,128)(2,1)}) %all-reduce.14.cloned.1.call-update) | async-done | bytes 66576 | tf_op jit(solution)/shard_map/while/body/eval_jaxpr/psum | solution.py:16
  429.3 3.0 bitcast_dynamic-update-slice_fusion.2
  433.1 20.5 all-reduce.8
  456.3 105.0 %all-reduce.14.cloned.1.call-done = bf16[2,16640]{1,0:T(2,128)(2,1)} async-done(((bf16[2,16640]{1,0:T(2,128)(2,1)}), bf16[2,16640]{1,0:T(2,128)(2,1)}) %all-reduce.14.cloned.1.call-update) | async-done | bytes 66576 | tf_op jit(solution)/shard_map/while/body/eval_jaxpr/psum | solution.py:16
  563.4 3.0 bitcast_dynamic-update-slice_fusion.2
  567.2 20.5 all-reduce.8
  590.4 104.9 %all-reduce.14.cloned.1.call-done = bf16[2,16640]{1,0:T(2,128)(2,1)} async-done(((bf16[2,16640]{1,0:T(2,128)(2,1)}), bf16[2,16640]{1,0:T(2,128)(2,1)}) %all-reduce.14.cloned.1.call-update) | async-done | bytes 66576 | tf_op jit(solution)/shard_map/while/body/eval_jaxpr/psum | solution.py:16
  701.2 20.5 all-reduce.8
  724.4 104.9 %all-reduce.14.cloned.1.call-done = bf16[2,16640]{1,0:T(2,128)(2,1)} async-done(((bf16[2,16640]{1,0:T(2,128)(2,1)}), bf16[2,16640]{1,0:T(2,128)(2,1)}) %all-reduce.14.cloned.1.call-update) | async-done | bytes 66576 | tf_op jit(solution)/shard_map/while/body/eval_jaxpr/psum | solution.py:16
  831.5 3.0 bitcast_dynamic-update-slice_fusion.2
  835.3 20.5 all-reduce.8
  858.4 105.3 %all-reduce.14.cloned.1.call-done = bf16[2,16640]{1,0:T(2,128)(2,1)} async-done(((bf16[2,16640]{1,0:T(2,128)(2,1)}), bf16[2,16640]{1,0:T(2,128)(2,1)}) %all-reduce.14.cloned.1.call-update) | async-done | bytes 66576 | tf_op jit(solution)/shard_map/while/body/eval_jaxpr/psum | solution.py:16
  965.8 3.0 bitcast_dynamic-update-slice_fusion.2
  969.7 20.5 all-reduce.8
  992.8 105.3 %all-reduce.14.cloned.1.call-done = bf16[2,16640]{1,0:T(2,128)(2,1)} async-done(((bf16[2,16640]{1,0:T(2,128)(2,1)}), bf16[2,16640]{1,0:T(2,128)(2,1)}) %all-reduce.14.cloned.1.call-update) | async-done | bytes 66576 | tf_op jit(solution)/shard_map/while/body/eval_jaxpr/psum | solution.py:16
  1104.0 20.5 all-reduce.8
  1127.2 105.3 %all-reduce.14.cloned.1.call-done = bf16[2,16640]{1,0:T(2,128)(2,1)} async-done(((bf16[2,16640]{1,0:T(2,128)(2,1)}), bf16[2,16640]{1,0:T(2,128)(2,1)}) %all-reduce.14.cloned.1.call-update) | async-done | bytes 66576 | tf_op jit(solution)/shard_map/while/body/eval_jaxpr/psum | solution.py:16
  1234.6 3.0 bitcast_dynamic-update-slice_fusion.2
  1238.4 20.5 all-reduce.8
  1261.5 105.0 %all-reduce.14.cloned.1.call-done = bf16[2,16640]{1,0:T(2,128)(2,1)} async-done(((bf16[2,16640]{1,0:T(2,128)(2,1)}), bf16[2,16640]{1,0:T(2,128)(2,1)}) %all-reduce.14.cloned.1.call-update) | async-done | bytes 66576 | tf_op jit(solution)/shard_map/while/body/eval_jaxpr/psum | solution.py:16
  1372.5 20.5 all-reduce.8
  1395.6 105.3 %all-reduce.14.cloned.1.call-done = bf16[2,16640]{1,0:T(2,128)(2,1)} async-done(((bf16[2,16640]{1,0:T(2,128)(2,1)}), bf16[2,16640]{1,0:T(2,128)(2,1)}) %all-reduce.14.cloned.1.call-update) | async-done | bytes 66576 | tf_op jit(solution)/shard_map/while/body/eval_jaxpr/psum | solution.py:16
  1503.0 3.0 bitcast_dynamic-update-slice_fusion.2
  1506.8 20.5 all-reduce.8
  1530.0 105.0 %all-reduce.14.cloned.1.call-done = bf16[2,16640]{1,0:T(2,128)(2,1)} async-done(((bf16[2,16640]{1,0:T(2,128)(2,1)}), bf16[2,16640]{1,0:T(2,128)(2,1)}) %all-reduce.14.cloned.1.call-update) | async-done | bytes 66576 | tf_op jit(solution)/shard_map/while/body/eval_jaxpr/psum | solution.py:16
  1640.9 20.5 all-reduce.8
  1664.0 105.3 %all-reduce.14.cloned.1.call-done = bf16[2,16640]{1,0:T(2,128)(2,1)} async-done(((bf16[2,16640]{1,0:T(2,128)(2,1)}), bf16[2,16640]{1,0:T(2,128)(2,1)}) %all-reduce.14.cloned.1.call-update) | async-done | bytes 66576 | tf_op jit(solution)/shard_map/while/body/eval_jaxpr/psum | solution.py:16
  1775.2 20.5 all-reduce.8
  1798.4 104.9 %all-reduce.14.cloned.1.call-done = bf16[2,16640]{1,0:T(2,128)(2,1)} async-done(((bf16[2,16640]{1,0:T(2,128)(2,1)}), bf16[2,16640]{1,0:T(2,128)(2,1)}) %all-reduce.14.cloned.1.call-update) | async-done | bytes 66576 | tf_op jit(solution)/shard_map/while/body/eval_jaxpr/psum | solution.py:16
  1905.4 3.0 bitcast_dynamic-update-slice_fusion.2
  1909.3 20.5 all-reduce.8
  1932.4 105.0 %all-reduce.14.cloned.1.call-done = bf16[2,16640]{1,0:T(2,128)(2,1)} async-done(((bf16[2,16640]{1,0:T(2,128)(2,1)}), bf16[2,16640]{1,0:T(2,128)(2,1)}) %all-reduce.14.cloned.1.call-update) | async-done | bytes 66576 | tf_op jit(solution)/shard_map/while/body/eval_jaxpr/psum | solution.py:16
  2039.5 3.0 bitcast_dynamic-update-slice_fusion.2
  2043.3 20.5 all-reduce.8
  2066.5 105.0 %all-reduce.14.cloned.1.call-done = bf16[2,16640]{1,0:T(2,128)(2,1)} async-done(((bf16[2,16640]{1,0:T(2,128)(2,1)}), bf16[2,16640]{1,0:T(2,128)(2,1)}) %all-reduce.14.cloned.1.call-update) | async-done | bytes 66576 | tf_op jit(solution)/shard_map/while/body/eval_jaxpr/psum | solution.py:16
  2173.6 3.0 bitcast_dynamic-update-slice_fusion.2
  2177.4 20.5 all-reduce.8
  2198.5 126.5 %while.89 = (s32[]{:T(128)}, f32[16,2,16640]{2,1,0:T(2,128)}, f32[16,2]{1,0:T(8,128)S(1)}, f32[16,8320]{1,0:T(8,128)S(1)}, s32[16]{0:T(128)S(1)}, /*index=5*/f32...) while((s32[]{:T(128)}, f32[16,2,16640]{2,1,0:T(2,128)}, ...), condition=%wide.region_12.13_spmd, body=%wide.region_8.12_spmd.sunk | while | flops 138461184 | bytes 10018055 | solution.py:132
  2201.0 3.8 fusion.45
  2208.9 3.8 fusion.45
  2216.8 3.8 fusion.45
  2224.7 3.8 fusion.45
  2232.6 3.8 fusion.45
  2240.5 3.8 fusion.45
  2248.4 3.8 fusion.45
  2256.3 3.8 fusion.45
  2264.3 3.8 fusion.45
  2272.2 3.8 fusion.45
  2280.1 3.8 fusion.45
  2288.0 3.8 fusion.45
  2295.9 3.8 fusion.45
  2303.8 3.8 fusion.45
  2311.7 3.8 fusion.45
  2319.6 3.8 fusion.45
  2326.2 31.8 %all-reduce.5 = f32[16,2]{1,0:T(8,128)S(1)} all-reduce(f32[16,2]{1,0:T(8,128)S(1)} %get-tuple-element.556), channel_id=5, replica_groups=mesh['dom'=16,'cls'=8] {'dom'}, use_global_device_ids=true, to_apply=%region_14.15.clone | all-reduce | flops 32 | bytes 256
  2359.1 87.3 %all-reduce.12.cloned.1.call-done = f32[16,2,16640]{2,1,0:T(2,128)} async-done(((f32[16,2,16640]{2,1,0:T(2,128)}), f32[16,2,16640]{2,1,0:T(2,128)}) %all-reduce.12.cloned.1.call-update) | async-done | bytes 2129936
  (552 shorter events, 139.6 us)
Async XLA Ops:
  28.6 17.1 copy-start
  28.6 17.1 copy-start.1
  28.6 17.1 copy-start.3
  28.6 17.1 copy-start.4
  28.6 17.1 copy-start.6
  45.7 112.7 %all-reduce.14.cloned.1.call-start = ((), (), s32[]{:S(2)}) async-start(), calls=%async_computation.1 | async-start | bytes 133120 | tf_op jit(solution)/shard_map/while/body/eval_jaxpr/psum | solution.py:16
  185.4 107.4 %all-reduce.14.cloned.1.call-start = ((), (), s32[]{:S(2)}) async-start(), calls=%async_computation.1 | async-start | bytes 133120 | tf_op jit(solution)/shard_map/while/body/eval_jaxpr/psum | solution.py:16
  319.8 107.4 %all-reduce.14.cloned.1.call-start = ((), (), s32[]{:S(2)}) async-start(), calls=%async_computation.1 | async-start | bytes 133120 | tf_op jit(solution)/shard_map/while/body/eval_jaxpr/psum | solution.py:16
  454.1 107.1 %all-reduce.14.cloned.1.call-start = ((), (), s32[]{:S(2)}) async-start(), calls=%async_computation.1 | async-start | bytes 133120 | tf_op jit(solution)/shard_map/while/body/eval_jaxpr/psum | solution.py:16
  588.2 107.1 %all-reduce.14.cloned.1.call-start = ((), (), s32[]{:S(2)}) async-start(), calls=%async_computation.1 | async-start | bytes 133120 | tf_op jit(solution)/shard_map/while/body/eval_jaxpr/psum | solution.py:16
  722.2 107.1 %all-reduce.14.cloned.1.call-start = ((), (), s32[]{:S(2)}) async-start(), calls=%async_computation.1 | async-start | bytes 133120 | tf_op jit(solution)/shard_map/while/body/eval_jaxpr/psum | solution.py:16
  856.3 107.4 %all-reduce.14.cloned.1.call-start = ((), (), s32[]{:S(2)}) async-start(), calls=%async_computation.1 | async-start | bytes 133120 | tf_op jit(solution)/shard_map/while/body/eval_jaxpr/psum | solution.py:16
  990.7 107.4 %all-reduce.14.cloned.1.call-start = ((), (), s32[]{:S(2)}) async-start(), calls=%async_computation.1 | async-start | bytes 133120 | tf_op jit(solution)/shard_map/while/body/eval_jaxpr/psum | solution.py:16
  1125.0 107.4 %all-reduce.14.cloned.1.call-start = ((), (), s32[]{:S(2)}) async-start(), calls=%async_computation.1 | async-start | bytes 133120 | tf_op jit(solution)/shard_map/while/body/eval_jaxpr/psum | solution.py:16
  1259.4 107.1 %all-reduce.14.cloned.1.call-start = ((), (), s32[]{:S(2)}) async-start(), calls=%async_computation.1 | async-start | bytes 133120 | tf_op jit(solution)/shard_map/while/body/eval_jaxpr/psum | solution.py:16
  1393.5 107.4 %all-reduce.14.cloned.1.call-start = ((), (), s32[]{:S(2)}) async-start(), calls=%async_computation.1 | async-start | bytes 133120 | tf_op jit(solution)/shard_map/while/body/eval_jaxpr/psum | solution.py:16
  1527.8 107.1 %all-reduce.14.cloned.1.call-start = ((), (), s32[]{:S(2)}) async-start(), calls=%async_computation.1 | async-start | bytes 133120 | tf_op jit(solution)/shard_map/while/body/eval_jaxpr/psum | solution.py:16
  1661.9 107.4 %all-reduce.14.cloned.1.call-start = ((), (), s32[]{:S(2)}) async-start(), calls=%async_computation.1 | async-start | bytes 133120 | tf_op jit(solution)/shard_map/while/body/eval_jaxpr/psum | solution.py:16
  1796.2 107.1 %all-reduce.14.cloned.1.call-start = ((), (), s32[]{:S(2)}) async-start(), calls=%async_computation.1 | async-start | bytes 133120 | tf_op jit(solution)/shard_map/while/body/eval_jaxpr/psum | solution.py:16
  1930.3 107.1 %all-reduce.14.cloned.1.call-start = ((), (), s32[]{:S(2)}) async-start(), calls=%async_computation.1 | async-start | bytes 133120 | tf_op jit(solution)/shard_map/while/body/eval_jaxpr/psum | solution.py:16
  2064.3 107.1 %all-reduce.14.cloned.1.call-start = ((), (), s32[]{:S(2)}) async-start(), calls=%async_computation.1 | async-start | bytes 133120 | tf_op jit(solution)/shard_map/while/body/eval_jaxpr/psum | solution.py:16
  2198.4 248.1 %all-reduce.12.cloned.1.call-start = ((), (), s32[]{:S(2)}) async-start(), calls=%async_computation | async-start | bytes 4259840
  2324.9 123.7 %copy-start.2 = (f32[16]{0:T(128)}, f32[16]{0:T(128)S(1)}, u32[]{:S(2)}) copy-start(f32[16]{0:T(128)S(1)} %get-tuple-element.1018) | copy-start | bytes 196
  2325.0 0.7 copy-start.5
Sparse Core Ops, SparseCore 0:
  49.8 108.6 all-reduce.13
  189.4 103.3 all-reduce.13
  323.8 103.3 all-reduce.13
  457.9 103.3 all-reduce.13
  591.9 103.3 all-reduce.13
  726.0 103.3 all-reduce.13
  860.3 103.3 all-reduce.13
  994.7 103.3 all-reduce.13
  1129.1 103.3 all-reduce.13
  1263.1 103.3 all-reduce.13
  1397.5 103.3 all-reduce.13
  1531.5 103.3 all-reduce.13
  1665.9 103.3 all-reduce.13
  1799.9 103.3 all-reduce.13
  1934.0 103.3 all-reduce.13
  2068.0 103.3 all-reduce.13
Sparse Core Ops, SparseCore 1:
  2325.1 121.3 all-reduce.11
where the time goes:
time: 2460 us
  waiting for transfers between devices  1770 us (72%)
  blocking collectives  360 us (15%)
  other arithmetic  115 us (5%)
  matrix products  110 us (4%)
  loops' own time  44.6 us (2%)
  local copies, waits for them, and re-layouts  35.7 us (1%)
    psum x16, waiting for transfers between devices, from_root(): return lax.psum(block, axis)  1690 us
    while x16, blocking collectives  328 us
    unnamed x2, waiting for transfers between devices  87.3 us
    dot_general x16, matrix products, project_back(): jnp.dot(posterior_floor.reshape(row_count * orient_count, trans_count), t...  61.1 us
  transfers between devices with their start and end apart: 17, of which 17 were waited for; matrix products, arithmetic and copies ran while one was open for 1% of the time, Pallas kernels for 0%

commit v1 on v0

v1 whole, which is shorter than its diff:
```python
import functools
import math

import jax
import jax.numpy as jnp
import numpy as np
from jax import lax
from jax.experimental import pallas as pl
from jax.experimental.pallas import tpu as pltpu
from jax.sharding import PartitionSpec as P

L = 128
LANES = 128
PRIOR_LOG_BOOST = 12.0
MESH = pl.DeviceIdType.MESH
F32 = jnp.float32
BF16 = jnp.bfloat16


class Sizes:
    def __init__(self, n_dom, n_cls, parts, orient, feat, orient_all):
        self.chips = n_dom // 2
        self.n_cls = n_cls
        self.parts = parts
        self.orient = orient
        self.orient_all = orient_all
        self.feat = feat
        self.tiles = feat // 2 // LANES
        self.chunks = 5
        self.per_chunk = self.tiles // self.chunks
        self.half_rows = self.per_chunk + 1
        self.row_stride = 2 * self.half_rows
        self.block = orient * self.row_stride
        self.refs = self.chips * orient
        self.imgs = 2 * parts
        self.rows = self.imgs * self.refs
        self.group = 2 * n_cls


def kernel(
    z,
    x_hbm,
    ref_ref,
    w_ref,
    shift_ref,
    pc_ref,
    po_ref,
    cos_ref,
    sin_ref,
    bp_ref,
    cw_ref,
    ln_ref,
    xb,
    x32,
    tab,
    prior,
    ref_rows,
    ref_send,
    ref_recv,
    ref_f32,
    acc,
    power,
    top,
    total,
    stats,
    scale,
    post,
    weight,
    back_rows,
    back_send,
    back_recv,
    back_own,
    back_sum,
    x_sem,
    pair_send,
    pair_recv,
    ref_ssem,
    ref_rsem,
    stat_ssem,
    stat_rsem,
    back_ssem,
    back_rsem,
):
    dom = lax.axis_index("dom")
    cls = lax.axis_index("cls")
    chip = dom // 2
    core = lax.rem(dom, 2)
    slot = cls * 2 + core
    other = 1 - core

    def same_core(step):
        peer_chip = lax.rem(chip + step, z.chips)
        return peer_chip, (peer_chip * 2 + core, cls)

    def same_images(step):
        peer = lax.rem(slot + step, z.group)
        return peer, (chip * 2 + lax.rem(peer, 2), peer // 2)

    barrier = pltpu.get_barrier_semaphore()

    def greet_refs(step, c):
        _, device = same_core(step)
        pl.semaphore_signal(barrier, inc=1, device_id=device, device_id_type=MESH)
        return c

    def greet_stats(step, c):
        _, device = same_images(step)
        pl.semaphore_signal(barrier, inc=1, device_id=device, device_id_type=MESH)
        return c

    lax.fori_loop(1, z.chips, greet_refs, 0)
    lax.fori_loop(1, z.group, greet_stats, 0)

    own_x = pltpu.make_async_copy(x_hbm, xb.at[core], x_sem)
    own_x.start()

    for tile in range(2 * z.tiles):
        part, kt = divmod(tile, z.tiles)
        s, k = divmod(kt, z.per_chunk)
        start = s * z.block + part * z.half_rows + k
        ref_rows[pl.ds(start, z.orient, stride=z.row_stride), :] = ref_ref[
            0, :, tile * LANES : (tile + 1) * LANES
        ].astype(F32)
    for s in range(z.chunks):
        rows = ref_rows[s * z.block : (s + 1) * z.block, :].astype(BF16)
        ref_send[s] = rows
        ref_recv[chip, s] = rows
    for i in range(z.parts):
        value = (pc_ref[i] * z.orient_all + po_ref[i]).astype(F32)
        prior[core, i : i + 1, :] = jnp.full((1, LANES), value, F32)

    pl.semaphore_wait(barrier, z.chips - 1 + z.group - 1)

    def pair_copies():
        device = (chip * 2 + other, cls)
        return (
            pltpu.make_async_remote_copy(
                src_ref=x_hbm,
                dst_ref=xb.at[core],
                send_sem=pair_send.at[0],
                recv_sem=pair_recv.at[0],
                device_id=device,
                device_id_type=MESH,
            ),
            pltpu.make_async_remote_copy(
                src_ref=prior.at[core],
                dst_ref=prior.at[core],
                send_sem=pair_send.at[1],
                recv_sem=pair_recv.at[1],
                device_id=device,
                device_id_type=MESH,
            ),
        )

    pair = pair_copies()
    for copy in pair:
        copy.start()

    def ref_copy(s, step):
        peer, device = same_core(step)
        return peer, pltpu.make_async_remote_copy(
            src_ref=ref_send.at[s],
            dst_ref=ref_recv.at[chip, s],
            send_sem=ref_ssem.at[step, s],
            recv_sem=ref_rsem.at[chip, s],
            device_id=device,
            device_id_type=MESH,
        )

    def ref_arrival(s, step):
        peer, device = same_core(step)
        return pltpu.make_async_remote_copy(
            src_ref=ref_send.at[s],
            dst_ref=ref_recv.at[peer, s],
            send_sem=ref_ssem.at[step, s],
            recv_sem=ref_rsem.at[peer, s],
            device_id=device,
            device_id_type=MESH,
        )

    def send_refs(s, c):
        def to_peer(step, c):
            ref_copy(s, step)[1].start()
            return c

        return lax.fori_loop(1, z.chips, to_peer, c)

    lax.fori_loop(0, z.chunks, send_refs, 0)

    shift_x = jnp.broadcast_to(shift_ref[:, 0:1].astype(F32), (LANES, LANES))
    shift_y = jnp.broadcast_to(shift_ref[:, 1:2].astype(F32), (LANES, LANES))
    lane = lax.broadcasted_iota(jnp.int32, (1, LANES), 1)
    half_width = L // 2 + 1

    def make_table(kt, c):
        k = kt * LANES + lane
        row = (k * 4033) >> 18
        col = k - row * half_width
        row = row.astype(F32)
        col = col.astype(F32)
        for t in range(0, LANES, 8):
            turn = (col * shift_x[t : t + 8] + row * shift_y[t : t + 8]).astype(jnp.int32) & (L - 1)
            cosine = jnp.take_along_axis(
                jnp.broadcast_to(cos_ref[...], (8, LANES)), turn, axis=1, mode="promise_in_bounds"
            )
            sine = jnp.take_along_axis(
                jnp.broadcast_to(sin_ref[...], (8, LANES)), turn, axis=1, mode="promise_in_bounds"
            )
            tab[kt, t : t + 8, :LANES] = cosine.astype(BF16)
            tab[kt, t : t + 8, LANES:] = sine.astype(BF16)
        return c

    lax.fori_loop(0, z.tiles, make_table, 0)

    own_x.wait()
    for copy in pair:
        copy.wait_recv()

    def widen(tile, c):
        at = pl.multiple_of(tile * LANES, LANES)
        to = pl.multiple_of(tile * z.imgs, 8)
        for half in range(2):
            x32[pl.ds(to + half * z.parts, z.parts), :] = xb[half, :, pl.ds(at, LANES)].astype(F32)
        return c

    lax.fori_loop(0, 2 * z.tiles, widen, 0)

    def image_row(tile, i):
        return x32[pl.ds(tile * z.imgs + i, 8, stride=0), :]

    halves = z.refs // 8
    acc[...] = jnp.zeros_like(acc)
    power[...] = jnp.zeros_like(power)

    def score_chunk(s, c):
        def arrive(step, c):
            ref_arrival(s, step).wait_recv()
            return c

        lax.fori_loop(1, z.chips, arrive, 0)
        for peer in range(z.chips):
            ref_f32[peer * z.block : (peer + 1) * z.block, :] = ref_recv[peer, s].astype(F32)

        def tile_step(k, c):
            kt = s * z.per_chunk + k
            noise = w_ref[pl.ds(kt, 8, stride=0), :]
            real, imag = [], []
            for h in range(halves):
                first = h * 8 * z.row_stride + k
                a_real = ref_f32[pl.ds(first, 8, stride=z.row_stride), :]
                a_imag = ref_f32[pl.ds(first + z.half_rows, 8, stride=z.row_stride), :]
                w_real = noise * a_real
                w_imag = noise * a_imag
                power[h * 8 : (h + 1) * 8, :] += w_real * a_real + w_imag * a_imag
                real.append(w_real)
                imag.append(w_imag)
            lhs = []
            for i in range(z.imgs):
                x_real = image_row(kt, i)
                x_imag = image_row(z.tiles + kt, i)
                p_real = jnp.concatenate(
                    [real[h] * x_real + imag[h] * x_imag for h in range(halves)], 0
                )
                p_imag = jnp.concatenate(
                    [real[h] * x_imag - imag[h] * x_real for h in range(halves)], 0
                )
                lhs.append(jnp.concatenate([p_real.astype(BF16), p_imag.astype(BF16)], 1))
            acc[...] += lax.dot_general(
                jnp.concatenate(lhs, 0),
                tab[kt],
                (((1,), (1,)), ((), ())),
                preferred_element_type=F32,
            )
            return c

        return lax.fori_loop(0, z.per_chunk, tile_step, c)

    lax.fori_loop(0, z.chunks, score_chunk, 0)

    row = lax.broadcasted_iota(jnp.int32, (z.refs, LANES), 0)
    class_id = 2 * (row // z.orient) + core
    ref_id = class_id * z.orient_all + cls * z.orient + lax.rem(row, z.orient)
    ref_id = ref_id.astype(F32)
    half_power = 0.5 * jnp.sum(power[...], axis=1, keepdims=True)
    for i in range(z.imgs):
        half, il = divmod(i, z.parts)
        block = acc[i * z.refs : (i + 1) * z.refs, :] - half_power
        block = block + jnp.where(prior[half, il : il + 1, :] == ref_id, PRIOR_LOG_BOOST, 0.0)
        acc[i * z.refs : (i + 1) * z.refs, :] = block
        top[i : i + 1, :] = jnp.max(block, axis=0, keepdims=True)
    top[...] = jnp.broadcast_to(jnp.max(top[...], axis=1, keepdims=True), top.shape)
    for i in range(z.imgs):
        block = jnp.exp(acc[i * z.refs : (i + 1) * z.refs, :] - top[i : i + 1, :])
        acc[i * z.refs : (i + 1) * z.refs, :] = block
        total[i : i + 1, :] = jnp.sum(block, axis=0, keepdims=True)
    sums = jnp.sum(total[...], axis=1, keepdims=True)
    lane8 = lax.broadcasted_iota(jnp.int32, (8, LANES), 1)
    groups = z.imgs // 8
    packed = jnp.zeros((8, LANES), F32)
    for v in range(groups):
        packed = jnp.where(lane8 == v, top[v * 8 : (v + 1) * 8, :], packed)
        packed = jnp.where(lane8 == groups + v, sums[v * 8 : (v + 1) * 8, :], packed)
    stats[slot] = packed

    def stat_copy(step):
        _, device = same_images(step)
        return pltpu.make_async_remote_copy(
            src_ref=stats.at[slot],
            dst_ref=stats.at[slot],
            send_sem=stat_ssem.at[step],
            recv_sem=stat_rsem.at[slot],
            device_id=device,
            device_id_type=MESH,
        )

    def stat_arrival(step):
        peer, device = same_images(step)
        return pltpu.make_async_remote_copy(
            src_ref=stats.at[peer],
            dst_ref=stats.at[peer],
            send_sem=stat_ssem.at[step],
            recv_sem=stat_rsem.at[peer],
            device_id=device,
            device_id_type=MESH,
        )

    def send_stat(step, c):
        stat_copy(step).start()
        return c

    def take_stat(step, c):
        stat_arrival(step).wait_recv()
        return c

    lax.fori_loop(1, z.group, send_stat, 0)
    lax.fori_loop(1, z.group, take_stat, 0)

    all_top = stats[0]
    for g in range(1, z.group):
        all_top = jnp.maximum(all_top, stats[g])
    all_total = jnp.zeros((8, LANES), F32)
    for g in range(z.group):
        part = stats[g]
        all_total = all_total + jnp.exp(part - all_top) * pltpu.roll(part, LANES - groups, 1)
    log_norm = all_top + jnp.log(all_total)
    rescale = jnp.exp(packed - log_norm)
    for v in range(groups):
        scale[v * 8 : (v + 1) * 8, :] = jnp.broadcast_to(rescale[:, v : v + 1], (8, LANES))
        total[v * 8 : (v + 1) * 8, :] = jnp.broadcast_to(log_norm[:, v : v + 1], (8, LANES))
    mine = total[pl.ds(pl.multiple_of(core * z.parts, 8), z.parts), :]
    diagonal = lax.broadcasted_iota(jnp.int32, (z.parts, LANES), 0) == lax.broadcasted_iota(
        jnp.int32, (z.parts, LANES), 1
    )
    ln_ref[...] = jnp.sum(jnp.where(diagonal, mine, 0.0), axis=0, keepdims=True)[:, : z.parts]

    mass = jnp.zeros((z.refs, LANES), F32)
    for i in range(z.imgs):
        block = acc[i * z.refs : (i + 1) * z.refs, :] * scale[i : i + 1, :]
        mass = mass + block
        post[i * z.refs : (i + 1) * z.refs, :] = block.astype(BF16)
    weight[...] = jnp.broadcast_to(jnp.sum(mass, axis=1, keepdims=True), weight.shape)

    def back_copy(s, step):
        peer, device = same_core(step)
        return pltpu.make_async_remote_copy(
            src_ref=back_send.at[peer, s],
            dst_ref=back_recv.at[chip, s],
            send_sem=back_ssem.at[step, s],
            recv_sem=back_rsem.at[chip, s],
            device_id=device,
            device_id_type=MESH,
        )

    def back_arrival(s, step):
        peer, device = same_core(step)
        return pltpu.make_async_remote_copy(
            src_ref=back_send.at[peer, s],
            dst_ref=back_recv.at[peer, s],
            send_sem=back_ssem.at[step, s],
            recv_sem=back_rsem.at[peer, s],
            device_id=device,
            device_id_type=MESH,
        )

    def back_chunk(s, c):
        def tile_step(k, c):
            kt = s * z.per_chunk + k
            coeff = jnp.dot(post[...], tab[kt], preferred_element_type=F32)
            real = [jnp.zeros((8, LANES), F32) for _ in range(halves)]
            imag = [jnp.zeros((8, LANES), F32) for _ in range(halves)]
            for i in range(z.imgs):
                x_real = image_row(kt, i)
                x_imag = image_row(z.tiles + kt, i)
                for h in range(halves):
                    at = i * z.refs + h * 8
                    cosine = coeff[at : at + 8, :LANES]
                    sine = coeff[at : at + 8, LANES:]
                    real[h] = real[h] + (x_real * cosine + x_imag * sine)
                    imag[h] = imag[h] + (x_imag * cosine - x_real * sine)
            for h in range(halves):
                first = h * 8 * z.row_stride + k
                back_rows[pl.ds(first, 8, stride=z.row_stride), :] = real[h]
                back_rows[pl.ds(first + z.half_rows, 8, stride=z.row_stride), :] = imag[h]
            return c

        lax.fori_loop(0, z.per_chunk, tile_step, 0)
        high = weight[...].astype(BF16).astype(F32)
        low = weight[...] - high
        for h in range(halves):
            first = h * 8 * z.row_stride + z.per_chunk
            rows = slice(h * 8, (h + 1) * 8)
            back_rows[pl.ds(first, 8, stride=z.row_stride), :] = high[rows]
            back_rows[pl.ds(first + z.half_rows, 8, stride=z.row_stride), :] = low[rows]
        for peer in range(z.chips):
            back_send[peer, s] = back_rows[peer * z.block : (peer + 1) * z.block, :].astype(BF16)
        back_own[s] = back_rows[pl.ds(pl.multiple_of(chip * z.block, 8), z.block), :]

        def to_peer(step, c):
            back_copy(s, step).start()
            return c

        return lax.fori_loop(1, z.chips, to_peer, c)

    lax.fori_loop(0, z.chunks, back_chunk, 0)

    def gather_chunk(s, c):
        def arrive(step, c):
            back_arrival(s, step).wait_recv()
            return c

        lax.fori_loop(1, z.chips, arrive, 0)

        def add(step, got):
            peer, _ = same_core(step)
            return got + back_recv[peer, s].astype(F32)

        back_sum[pl.ds(pl.multiple_of(s * z.block, 8), z.block), :] = lax.fori_loop(
            1, z.chips, add, back_own[s]
        )
        return c

    lax.fori_loop(0, z.chunks, gather_chunk, 0)
    for tile in range(2 * z.tiles):
        part, kt = divmod(tile, z.tiles)
        s, k = divmod(kt, z.per_chunk)
        start = s * z.block + part * z.half_rows + k
        bp_ref[0, :, tile * LANES : (tile + 1) * LANES] = back_sum[
            pl.ds(start, z.orient, stride=z.row_stride), :
        ]
    line = jnp.zeros((1, LANES), F32)
    for o in range(z.orient):
        at = o * z.row_stride + z.per_chunk
        both = back_sum[at : at + 1, :] + back_sum[at + z.half_rows : at + z.half_rows + 1, :]
        line = jnp.where(lane == o, both, line)
    cw_ref[...] = line[:, : z.orient]

    for copy in pair:
        copy.wait_send()

    def drain_chunk(s, c):
        def drain(step, c):
            ref_copy(s, step)[1].wait_send()
            back_copy(s, step).wait_send()
            return c

        return lax.fori_loop(1, z.chips, drain, c)

    def drain_stat(step, c):
        stat_copy(step).wait_send()
        return c

    lax.fori_loop(0, z.chunks, drain_chunk, 0)
    lax.fori_loop(1, z.group, drain_stat, 0)


def on_device(z, particles, references, inv_noise, shifts, prior_class, prior_orient):
    angle = (np.arange(L, dtype=np.float32) * np.float32(2.0 * math.pi / L)).astype(np.float64)
    cosine = jnp.asarray(np.cos(angle).astype(np.float32)[None])
    sine = jnp.asarray(np.sin(angle).astype(np.float32)[None])
    vmem = pl.BlockSpec(memory_space=pltpu.VMEM)
    smem = pl.BlockSpec(memory_space=pltpu.SMEM)
    dma = pltpu.SemaphoreType.DMA
    blocks = (z.chips, z.chunks, z.block, LANES)
    flops = 4 * z.rows * z.feat * LANES
    bp, cw, ln = pl.pallas_call(
        functools.partial(kernel, z),
        out_shape=(
            jax.ShapeDtypeStruct((1, z.orient, z.feat), F32),
            jax.ShapeDtypeStruct((1, z.orient), F32),
            jax.ShapeDtypeStruct((1, z.parts), F32),
        ),
        in_specs=[pl.BlockSpec(memory_space=pl.ANY), vmem, vmem, vmem, smem, smem, vmem, vmem],
        out_specs=(vmem, vmem, vmem),
        scratch_shapes=[
            pltpu.VMEM((2, z.parts, z.feat), BF16),
            pltpu.VMEM((2 * z.tiles * z.imgs, LANES), F32),
            pltpu.VMEM((z.tiles, LANES, 2 * LANES), BF16),
            pltpu.VMEM((2, z.parts, LANES), F32),
            pltpu.VMEM((z.chunks * z.block, LANES), F32),
            pltpu.VMEM((z.chunks, z.block, LANES), BF16),
            pltpu.VMEM(blocks, BF16),
            pltpu.VMEM((z.chips * z.block, LANES), F32),
            pltpu.VMEM((z.rows, LANES), F32),
            pltpu.VMEM((z.refs, LANES), F32),
            pltpu.VMEM((z.imgs, LANES), F32),
            pltpu.VMEM((z.imgs, LANES), F32),
            pltpu.VMEM((z.group, 8, LANES), F32),
            pltpu.VMEM((z.imgs, LANES), F32),
            pltpu.VMEM((z.rows, LANES), BF16),
            pltpu.VMEM((z.refs, LANES), F32),
            pltpu.VMEM((z.chips * z.block, LANES), F32),
            pltpu.VMEM(blocks, BF16),
            pltpu.VMEM(blocks, BF16),
            pltpu.VMEM((z.chunks, z.block, LANES), F32),
            pltpu.VMEM((z.chunks * z.block, LANES), F32),
            dma,
            dma((2,)),
            dma((2,)),
            dma((z.chips, z.chunks)),
            dma((z.chips, z.chunks)),
            dma((z.group,)),
            dma((z.group,)),
            dma((z.chips, z.chunks)),
            dma((z.chips, z.chunks)),
        ],
        compiler_params=pltpu.CompilerParams(
            collective_id=0, has_side_effects=True, vmem_limit_bytes=40 * 2**20
        ),
        cost_estimate=pl.CostEstimate(
            flops=flops, bytes_accessed=4 * 2**20, transcendentals=z.rows * LANES
        ),
    )(
        particles,
        references,
        inv_noise.reshape(z.tiles, LANES),
        shifts,
        prior_class,
        prior_orient,
        cosine,
        sine,
    )
    return bp, cw, ln.reshape(z.parts)


def solution(mesh):
    def body(particles, references, inv_noise, shifts, prior_class, prior_orient):
        n_dom, n_cls = lax.axis_size("dom"), lax.axis_size("cls")
        z = Sizes(
            n_dom,
            n_cls,
            particles.shape[0],
            references.shape[1],
            particles.shape[1],
            references.shape[1] * n_cls,
        )
        return on_device(z, particles, references, inv_noise, shifts, prior_class, prior_orient)

    placed = (P("dom", None), P("dom", "cls", None), P(), P(), P("dom"), P("dom"))
    return jax.shard_map(
        body,
        mesh=mesh,
        in_specs=placed,
        out_specs=(P("dom", "cls", None), P("dom", "cls"), P("dom")),
        check_vma=False,
    )
```

time: 2460 us -> 71.6 us (0.03)
  waiting for transfers between devices: 1770 us -> 0 us
  blocking collectives: 360 us -> 0 us
  other arithmetic: 115 us -> 0 us
  matrix products: 110 us -> 0 us
  Pallas kernels: 0 us -> 65.6 us
  loops' own time: 44.6 us -> 0 us
  local copies, waits for them, and re-layouts: 35.7 us -> 5 us
    psum x16 -> x0, waiting for transfers between devices: 1690 us -> none  [from_root(): return lax.psum(block, axis)]
    while x16 -> x0, blocking collectives: 328 us -> none
    dot_general x32 -> x0, matrix products: 110 us -> none  [the longest x16 61.1 us: project_back(): jnp.dot(posterior_floor.reshape(row_count * orient_count, trans_count), t...]
    unnamed x2 -> x0, waiting for transfers between devices: 87.3 us -> none
    pallas_call x0 -> x1, Pallas kernels: none -> 65.6 us  [on_device(): pl.pallas_call(functools.partial(kernel, z), out_shape=(jax.ShapeDtypeStr...]
    another operation x18 -> x0, loops' own time: 44.6 us -> none  [the longest x1 31.3 us: on_device(): lax.map(back_class, jnp.arange(classes, dtype=jnp.int32))]
    unnamed x1 -> x0, blocking collectives: 31.8 us -> none
    reduce_sum x64 -> x0, other arithmetic: 31.2 us -> none  [the longest x16 15.3 us: correlate(): jnp.sum(inv_noise * (ref_real * ref_real + ref_imag * ref_imag), -1)]
  transfers between devices with their start and end apart: 17 -> 0, of which waited for: 17 -> 0; matrix products, arithmetic and copies ran while one was open for 1% -> 0% of each run, Pallas kernels for 0% -> 0%
where the time goes in v1:
time: 71.6 us; the launch traced here: 71.3 us
  Pallas kernels  65.6 us (92%)
  local copies, waits for them, and re-layouts  5 us (7%)
    pallas_call x1, Pallas kernels, on_device(): pl.pallas_call(functools.partial(kernel, z), out_shape=(jax.ShapeDtypeStr...  65.6 us
    unnamed x18, local copies, waits for them, and re-layouts  5 us

profile of v1, /device:TPU:1, one launch (start us, length us, event | category | flops | bytes accessed | tf_op | source)
XLA Modules:
  0.0 71.3 jit_solution(7248191269288141687)
XLA Ops:
  0.6 0.0 copy-start.1
  0.6 0.0 copy-start.3
  0.7 0.0 copy-start.4
  0.7 0.0 copy-start.5
  0.7 0.8 %copy.11.shift_ref = s32[128,2]{1,0:T(8,128)S(1)} copy(s32[128,2]{0,1:T(2,128)} %param.11) | data formatting | bytes 2048 | tf_op args[3]
  1.5 0.0 copy-done.1
  1.5 0.0 copy-done.3
  1.5 0.0 copy-done.4
  1.5 0.0 copy-done.5
  1.5 0.0 copy-start
  1.5 1.0 %copy-done = bf16[16,16640]{1,0:T(8,128)(2,1)S(1)} copy-done((bf16[16,16640]{1,0:T(8,128)(2,1)S(1)}, bf16[16,16640]{1,0:T(8,128)(2,1)}, u32[]{:S(2)}) %copy-start) | copy-done | bytes 532504
  2.6 0.0 copy-start.2
  2.6 0.8 %copy-done.2 = f32[8320]{0:T(1024)S(1)} copy-done((f32[8320]{0:T(1024)S(1)}, f32[8320]{0:T(1024)}, u32[]{:S(2)}) %copy-start.2) | copy-done | bytes 33304
  3.3 0.0 copy-start.6
  3.3 0.7 copy-done.6
  4.0 65.6 %shard_map.103 = (f32[1,2,16640]{2,1,0:T(2,128)S(1)}, f32[1,2]{1,0:T(1,128)S(1)}, f32[1,16]{1,0:T(1,128)S(1)}) custom-call(bf16[16,16640]{1,0:T(8,128)(2,1)S(1)} %copy-done, bf16[1,2,16640]{2,1,0:T(2,128)(2,1)S(1)} %copy-done.1, f32[65,128]{1,0:T(8,128)S(1)} %bitcast.2, s32[128,2]{1,0:T(8,128)S(1)} %copy.11.shift_ref, s32[16]{0:T(128)S(1)} %copy-done.3, ...), custom_call_target="tpu_custom_call" | custom-call | flops 4362076160 | bytes 4194304 | tf_op jit(solution)/shard_map/pallas_call | solution.py:485
  69.6 0.7 copy.15
  70.3 0.5 copy.16
  70.8 0.5 copy.17
Async XLA Ops:
  0.6 0.9 %copy-start.1 = (bf16[1,2,16640]{2,1,0:T(2,128)(2,1)S(1)}, bf16[1,2,16640]{2,1,0:T(2,128)(2,1)}, u32[]{:S(2)}) copy-start(bf16[1,2,16640]{2,1,0:T(2,128)(2,1)} %ref_ref.1) | copy-start | bytes 199684
  0.6 0.9 %copy-start.3 = (s32[16]{0:T(128)S(1)}, s32[16]{0:T(128)}, u32[]{:S(2)}) copy-start(s32[16]{0:T(128)} %pc_ref.1) | copy-start | bytes 196
  0.7 0.9 %copy-start.4 = (s32[16]{0:T(128)S(1)}, s32[16]{0:T(128)}, u32[]{:S(2)}) copy-start(s32[16]{0:T(128)} %po_ref.1) | copy-start | bytes 196
  0.7 0.9 %copy-start.5 = (f32[1,128]{1,0:T(1,128)S(1)}, f32[1,128]{1,0:T(1,128)}, u32[]{:S(2)}) copy-start(f32[1,128]{1,0:T(1,128)} %constant.5.clone.sin_ref) | copy-start | bytes 1540
  1.5 1.0 %copy-start = (bf16[16,16640]{1,0:T(8,128)(2,1)S(1)}, bf16[16,16640]{1,0:T(8,128)(2,1)}, u32[]{:S(2)}) copy-start(bf16[16,16640]{1,0:T(8,128)(2,1)} %x_hbm.1) | copy-start | bytes 1597444
  2.6 0.8 %copy-start.2 = (f32[8320]{0:T(1024)S(1)}, f32[8320]{0:T(1024)}, u32[]{:S(2)}) copy-start(f32[8320]{0:T(1024)} %param.10) | copy-start | bytes 99844
  3.3 0.7 copy-start.6

commit v2 on v1

--- a/solution.py
+++ b/solution.py
@@ -187,30 +187,64 @@
 
     lax.fori_loop(0, z.chunks, send_refs, 0)
 
-    shift_x = jnp.broadcast_to(shift_ref[:, 0:1].astype(F32), (LANES, LANES))
-    shift_y = jnp.broadcast_to(shift_ref[:, 1:2].astype(F32), (LANES, LANES))
     lane = lax.broadcasted_iota(jnp.int32, (1, LANES), 1)
     half_width = L // 2 + 1
 
-    def make_table(kt, c):
-        k = kt * LANES + lane
-        row = (k * 4033) >> 18
-        col = k - row * half_width
-        row = row.astype(F32)
-        col = col.astype(F32)
-        for t in range(0, LANES, 8):
-            turn = (col * shift_x[t : t + 8] + row * shift_y[t : t + 8]).astype(jnp.int32) & (L - 1)
-            cosine = jnp.take_along_axis(
-                jnp.broadcast_to(cos_ref[...], (8, LANES)), turn, axis=1, mode="promise_in_bounds"
+    def look_up(turn):
+        turn = turn.astype(jnp.int32) & (L - 1)
+        return tuple(
+            jnp.take_along_axis(
+                jnp.broadcast_to(ref[...], (8, LANES)), turn, axis=1, mode="promise_in_bounds"
             )
-            sine = jnp.take_along_axis(
-                jnp.broadcast_to(sin_ref[...], (8, LANES)), turn, axis=1, mode="promise_in_bounds"
+            for ref in (cos_ref, sin_ref)
+        )
+
+    lane8 = lax.broadcasted_iota(jnp.int32, (8, LANES), 1)
+    first_row = jnp.where(lane8 >= half_width, 1, 0)
+    first_col = lane8 - half_width * first_row
+    rows_on, rows_over = divmod(LANES, half_width)
+    rows_on, rows_back = rows_on + 1, half_width - rows_over
+    span = 8
+    for t0 in range(0, LANES, 8 * span):
+        start, turns = [], []
+        for v in range(span):
+            rows = slice(t0 + 8 * v, t0 + 8 * v + 8)
+            shift_x = jnp.broadcast_to(shift_ref[rows, 0:1].astype(F32), (8, LANES))
+            shift_y = jnp.broadcast_to(shift_ref[rows, 1:2].astype(F32), (8, LANES))
+            start.append(
+                look_up(first_col.astype(F32) * shift_x + first_row.astype(F32) * shift_y)
             )
-            tab[kt, t : t + 8, :LANES] = cosine.astype(BF16)
-            tab[kt, t : t + 8, LANES:] = sine.astype(BF16)
-        return c
-
-    lax.fori_loop(0, z.tiles, make_table, 0)
+            turns.append(
+                (
+                    look_up(rows_on * shift_y - rows_back * shift_x),
+                    look_up((rows_on - 1) * shift_y + rows_over * shift_x),
+                )
+            )
+
+        def make_table(step, carry):
+            now, col = carry
+            for j in range(z.per_chunk):
+                kt = step * z.per_chunk + j
+                near = col >= rows_back
+                col = jnp.where(near, col - rows_back, col + rows_over)
+                after = []
+                for v in range(span):
+                    cosine, sine = now[v]
+                    rows = slice(t0 + 8 * v, t0 + 8 * v + 8)
+                    tab[kt, rows, :LANES] = cosine.astype(BF16)
+                    tab[kt, rows, LANES:] = sine.astype(BF16)
+                    turn_cos = jnp.where(near, turns[v][0][0], turns[v][1][0])
+                    turn_sin = jnp.where(near, turns[v][0][1], turns[v][1][1])
+                    after.append(
+                        (
+                            cosine * turn_cos - sine * turn_sin,
+                            sine * turn_cos + cosine * turn_sin,
+                        )
+                    )
+                now = tuple(after)
+            return now, col
+
+        lax.fori_loop(0, z.chunks, make_table, (tuple(start), first_col))
 
     own_x.wait()
     for copy in pair:
@@ -241,7 +275,7 @@
         for peer in range(z.chips):
             ref_f32[peer * z.block : (peer + 1) * z.block, :] = ref_recv[peer, s].astype(F32)
 
-        def tile_step(k, c):
+        def tile_step(k):
             kt = s * z.per_chunk + k
             noise = w_ref[pl.ds(kt, 8, stride=0), :]
             real, imag = [], []
@@ -271,9 +305,10 @@
                 (((1,), (1,)), ((), ())),
                 preferred_element_type=F32,
             )
-            return c
-
-        return lax.fori_loop(0, z.per_chunk, tile_step, c)
+
+        for k in range(z.per_chunk):
+            tile_step(k)
+        return c
 
     lax.fori_loop(0, z.chunks, score_chunk, 0)
 
@@ -294,7 +329,6 @@
         acc[i * z.refs : (i + 1) * z.refs, :] = block
         total[i : i + 1, :] = jnp.sum(block, axis=0, keepdims=True)
     sums = jnp.sum(total[...], axis=1, keepdims=True)
-    lane8 = lax.broadcasted_iota(jnp.int32, (8, LANES), 1)
     groups = z.imgs // 8
     packed = jnp.zeros((8, LANES), F32)
     for v in range(groups):
@@ -383,7 +417,7 @@
         )
 
     def back_chunk(s, c):
-        def tile_step(k, c):
+        def tile_step(k):
             kt = s * z.per_chunk + k
             coeff = jnp.dot(post[...], tab[kt], preferred_element_type=F32)
             real = [jnp.zeros((8, LANES), F32) for _ in range(halves)]
@@ -401,9 +435,9 @@
                 first = h * 8 * z.row_stride + k
                 back_rows[pl.ds(first, 8, stride=z.row_stride), :] = real[h]
                 back_rows[pl.ds(first + z.half_rows, 8, stride=z.row_stride), :] = imag[h]
-            return c
-
-        lax.fori_loop(0, z.per_chunk, tile_step, 0)
+
+        for k in range(z.per_chunk):
+            tile_step(k)
         high = weight[...].astype(BF16).astype(F32)
         low = weight[...] - high
         for h in range(halves):

time: 71.6 us -> 42.3 us (0.59)
  Pallas kernels: 65.6 us -> 36.3 us
    pallas_call x1, Pallas kernels: 65.6 us -> 36.3 us  [on_device(): pl.pallas_call(functools.partial(kernel, z), out_shape=(jax.ShapeDtypeStr...]
where the time goes in v2:
time: 42.3 us; the launch traced here: 42 us
  Pallas kernels  36.3 us (86%)
  local copies, waits for them, and re-layouts  5 us (12%)
  between operations  0.69 us (2%)
    pallas_call x1, Pallas kernels, on_device(): pl.pallas_call(functools.partial(kernel, z), out_shape=(jax.ShapeDtypeStr...  36.3 us
    unnamed x18, local copies, waits for them, and re-layouts  5 us

profile of v2, /device:TPU:1, one launch (start us, length us, event | category | flops | bytes accessed | tf_op | source)
XLA Modules:
  0.0 42.0 jit_solution(16671658726328511151)
XLA Ops:
  0.6 0.0 copy-start.1
  0.6 0.0 copy-start.3
  0.7 0.0 copy-start.4
  0.7 0.0 copy-start.5
  0.7 0.8 %copy.11.shift_ref = s32[128,2]{1,0:T(8,128)S(1)} copy(s32[128,2]{0,1:T(2,128)} %param.11) | data formatting | bytes 2048 | tf_op args[3]
  1.5 0.0 copy-done.1
  1.5 0.0 copy-done.3
  1.5 0.0 copy-done.4
  1.5 0.0 copy-done.5
  1.5 0.0 copy-start
  1.5 1.0 %copy-done = bf16[16,16640]{1,0:T(8,128)(2,1)S(1)} copy-done((bf16[16,16640]{1,0:T(8,128)(2,1)S(1)}, bf16[16,16640]{1,0:T(8,128)(2,1)}, u32[]{:S(2)}) %copy-start) | copy-done | bytes 532504
  2.6 0.0 copy-start.2
  2.6 0.8 %copy-done.2 = f32[8320]{0:T(1024)S(1)} copy-done((f32[8320]{0:T(1024)S(1)}, f32[8320]{0:T(1024)}, u32[]{:S(2)}) %copy-start.2) | copy-done | bytes 33304
  3.3 0.0 copy-start.6
  3.3 0.7 %copy-done.6 = f32[1,128]{1,0:T(1,128)S(1)} copy-done((f32[1,128]{1,0:T(1,128)S(1)}, f32[1,128]{1,0:T(1,128)}, u32[]{:S(2)}) %copy-start.6) | copy-done | bytes 536
  4.0 36.3 %shard_map.103 = (f32[1,2,16640]{2,1,0:T(2,128)S(1)}, f32[1,2]{1,0:T(1,128)S(1)}, f32[1,16]{1,0:T(1,128)S(1)}) custom-call(bf16[16,16640]{1,0:T(8,128)(2,1)S(1)} %copy-done, bf16[1,2,16640]{2,1,0:T(2,128)(2,1)S(1)} %copy-done.1, f32[65,128]{1,0:T(8,128)S(1)} %bitcast.2, s32[128,2]{1,0:T(8,128)S(1)} %copy.11.shift_ref, s32[16]{0:T(128)S(1)} %copy-done.3, ...), custom_call_target="tpu_custom_call" | custom-call | flops 4362076160 | bytes 4194304 | tf_op jit(solution)/shard_map/pallas_call | solution.py:519
  40.3 0.7 %copy.15 = f32[1,2,16640]{2,1,0:T(2,128)} copy(f32[1,2,16640]{2,1,0:T(2,128)S(1)} %get-tuple-element.12) | data formatting | bytes 266240
  41.0 0.5 %copy.16 = f32[1,2]{1,0:T(1,128)} copy(f32[1,2]{1,0:T(1,128)S(1)} %get-tuple-element.13) | data formatting | bytes 16
  41.5 0.5 %copy.17 = f32[16]{0:T(128)} copy(f32[16]{0:T(128)S(1)} %bitcast.3) | data formatting | bytes 128
Async XLA Ops:
  0.6 0.9 %copy-start.1 = (bf16[1,2,16640]{2,1,0:T(2,128)(2,1)S(1)}, bf16[1,2,16640]{2,1,0:T(2,128)(2,1)}, u32[]{:S(2)}) copy-start(bf16[1,2,16640]{2,1,0:T(2,128)(2,1)} %ref_ref.1) | copy-start | bytes 199684
  0.6 0.9 %copy-start.3 = (s32[16]{0:T(128)S(1)}, s32[16]{0:T(128)}, u32[]{:S(2)}) copy-start(s32[16]{0:T(128)} %pc_ref.1) | copy-start | bytes 196
  0.7 0.9 %copy-start.4 = (s32[16]{0:T(128)S(1)}, s32[16]{0:T(128)}, u32[]{:S(2)}) copy-start(s32[16]{0:T(128)} %po_ref.1) | copy-start | bytes 196
  0.7 0.9 %copy-start.5 = (f32[1,128]{1,0:T(1,128)S(1)}, f32[1,128]{1,0:T(1,128)}, u32[]{:S(2)}) copy-start(f32[1,128]{1,0:T(1,128)} %constant.5.clone.sin_ref) | copy-start | bytes 1540
  1.5 1.0 %copy-start = (bf16[16,16640]{1,0:T(8,128)(2,1)S(1)}, bf16[16,16640]{1,0:T(8,128)(2,1)}, u32[]{:S(2)}) copy-start(bf16[16,16640]{1,0:T(8,128)(2,1)} %x_hbm.1) | copy-start | bytes 1597444
  2.6 0.8 %copy-start.2 = (f32[8320]{0:T(1024)S(1)}, f32[8320]{0:T(1024)}, u32[]{:S(2)}) copy-start(f32[8320]{0:T(1024)} %param.10) | copy-start | bytes 99844
  3.3 0.7 %copy-start.6 = (f32[1,128]{1,0:T(1,128)S(1)}, f32[1,128]{1,0:T(1,128)}, u32[]{:S(2)}) copy-start(f32[1,128]{1,0:T(1,128)} %constant.4.clone.cos_ref) | copy-start | bytes 1540

commit v3 on v2

--- a/solution.py
+++ b/solution.py
@@ -40,16 +40,20 @@
 def kernel(
     z,
     x_hbm,
+    ref_hbm,
+    w_hbm,
+    shift_hbm,
+    pc_hbm,
+    po_hbm,
+    circle_hbm,
+    sum_ref,
+    ln_ref,
     ref_ref,
     w_ref,
     shift_ref,
     pc_ref,
     po_ref,
-    cos_ref,
-    sin_ref,
-    bp_ref,
-    cw_ref,
-    ln_ref,
+    circle_ref,
     xb,
     x32,
     tab,
@@ -70,8 +74,8 @@
     back_send,
     back_recv,
     back_own,
-    back_sum,
     x_sem,
+    in_sem,
     pair_send,
     pair_recv,
     ref_ssem,
@@ -88,6 +92,24 @@
     slot = cls * 2 + core
     other = 1 - core
 
+    own_x = pltpu.make_async_copy(x_hbm, xb.at[core], x_sem)
+    small = [
+        pltpu.make_async_copy(src, dst, in_sem.at[n])
+        for n, (src, dst) in enumerate(
+            (
+                (ref_hbm, ref_ref),
+                (pc_hbm, pc_ref),
+                (po_hbm, po_ref),
+                (shift_hbm, shift_ref),
+                (circle_hbm, circle_ref),
+                (w_hbm, w_ref),
+            )
+        )
+    ]
+    for copy in small:
+        copy.start()
+    own_x.start()
+
     def same_core(step):
         peer_chip = lax.rem(chip + step, z.chips)
         return peer_chip, (peer_chip * 2 + core, cls)
@@ -111,8 +133,8 @@
     lax.fori_loop(1, z.chips, greet_refs, 0)
     lax.fori_loop(1, z.group, greet_stats, 0)
 
-    own_x = pltpu.make_async_copy(x_hbm, xb.at[core], x_sem)
-    own_x.start()
+    for copy in small:
+        copy.wait()
 
     for tile in range(2 * z.tiles):
         part, kt = divmod(tile, z.tiles)
@@ -196,10 +218,12 @@
             jnp.take_along_axis(
                 jnp.broadcast_to(ref[...], (8, LANES)), turn, axis=1, mode="promise_in_bounds"
             )
-            for ref in (cos_ref, sin_ref)
+            for ref in (circle_ref.at[0:1], circle_ref.at[1:2])
         )
 
     lane8 = lax.broadcasted_iota(jnp.int32, (8, LANES), 1)
+    sub8 = lax.broadcasted_iota(jnp.int32, (8, LANES), 0)
+    shift_rows = shift_ref[...].astype(F32)
     first_row = jnp.where(lane8 >= half_width, 1, 0)
     first_col = lane8 - half_width * first_row
     rows_on, rows_over = divmod(LANES, half_width)
@@ -209,8 +233,18 @@
         start, turns = [], []
         for v in range(span):
             rows = slice(t0 + 8 * v, t0 + 8 * v + 8)
-            shift_x = jnp.broadcast_to(shift_ref[rows, 0:1].astype(F32), (8, LANES))
-            shift_y = jnp.broadcast_to(shift_ref[rows, 1:2].astype(F32), (8, LANES))
+            here = lane8 - sub8 == rows.start
+            shift_x, shift_y = (
+                jnp.broadcast_to(
+                    jnp.sum(
+                        jnp.where(here, jnp.broadcast_to(shift_rows[n : n + 1, :], (8, LANES)), 0.0),
+                        axis=1,
+                        keepdims=True,
+                    ),
+                    (8, LANES),
+                )
+                for n in range(2)
+            )
             start.append(
                 look_up(first_col.astype(F32) * shift_x + first_row.astype(F32) * shift_y)
             )
@@ -385,7 +419,7 @@
     diagonal = lax.broadcasted_iota(jnp.int32, (z.parts, LANES), 0) == lax.broadcasted_iota(
         jnp.int32, (z.parts, LANES), 1
     )
-    ln_ref[...] = jnp.sum(jnp.where(diagonal, mine, 0.0), axis=0, keepdims=True)[:, : z.parts]
+    ln_ref[...] = jnp.sum(jnp.where(diagonal, mine, 0.0), axis=0, keepdims=True)
 
     mass = jnp.zeros((z.refs, LANES), F32)
     for i in range(z.imgs):
@@ -468,64 +502,83 @@
             peer, _ = same_core(step)
             return got + back_recv[peer, s].astype(F32)
 
-        back_sum[pl.ds(pl.multiple_of(s * z.block, 8), z.block), :] = lax.fori_loop(
+        sum_ref[pl.ds(pl.multiple_of(s * z.block, 8), z.block), :] = lax.fori_loop(
             1, z.chips, add, back_own[s]
         )
         return c
 
     lax.fori_loop(0, z.chunks, gather_chunk, 0)
+    for copy in pair:
+        copy.wait_send()
+
+    def drain_chunk(s, c):
+        def drain(step, c):
+            ref_copy(s, step)[1].wait_send()
+            back_copy(s, step).wait_send()
+            return c
+
+        return lax.fori_loop(1, z.chips, drain, c)
+
+    def drain_stat(step, c):
+        stat_copy(step).wait_send()
+        return c
+
+    lax.fori_loop(0, z.chunks, drain_chunk, 0)
+    lax.fori_loop(1, z.group, drain_stat, 0)
+
+
+def finish(z, sum_ref, ln_ref, bp_ref, cw_ref, lnorm_ref, bp_buf, cw_buf, ln_buf, sem):
+    lane = lax.broadcasted_iota(jnp.int32, (1, LANES), 1)
     for tile in range(2 * z.tiles):
         part, kt = divmod(tile, z.tiles)
         s, k = divmod(kt, z.per_chunk)
         start = s * z.block + part * z.half_rows + k
-        bp_ref[0, :, tile * LANES : (tile + 1) * LANES] = back_sum[
+        bp_buf[0, :, tile * LANES : (tile + 1) * LANES] = sum_ref[
             pl.ds(start, z.orient, stride=z.row_stride), :
         ]
     line = jnp.zeros((1, LANES), F32)
     for o in range(z.orient):
         at = o * z.row_stride + z.per_chunk
-        both = back_sum[at : at + 1, :] + back_sum[at + z.half_rows : at + z.half_rows + 1, :]
+        both = sum_ref[at : at + 1, :] + sum_ref[at + z.half_rows : at + z.half_rows + 1, :]
         line = jnp.where(lane == o, both, line)
-    cw_ref[...] = line[:, : z.orient]
-
-    for copy in pair:
-        copy.wait_send()
-
-    def drain_chunk(s, c):
-        def drain(step, c):
-            ref_copy(s, step)[1].wait_send()
-            back_copy(s, step).wait_send()
-            return c
-
-        return lax.fori_loop(1, z.chips, drain, c)
-
-    def drain_stat(step, c):
-        stat_copy(step).wait_send()
-        return c
-
-    lax.fori_loop(0, z.chunks, drain_chunk, 0)
-    lax.fori_loop(1, z.group, drain_stat, 0)
+    cw_buf[...] = line[:, : z.orient]
+
+    ln_buf[...] = ln_ref[:, : z.parts]
+    copies = [
+        pltpu.make_async_copy(src, dst, sem.at[n])
+        for n, (src, dst) in enumerate(
+            ((bp_buf, bp_ref), (cw_buf, cw_ref), (ln_buf, lnorm_ref))
+        )
+    ]
+    for copy in copies:
+        copy.start()
+    for copy in copies:
+        copy.wait()
 
 
 def on_device(z, particles, references, inv_noise, shifts, prior_class, prior_orient):
     angle = (np.arange(L, dtype=np.float32) * np.float32(2.0 * math.pi / L)).astype(np.float64)
-    cosine = jnp.asarray(np.cos(angle).astype(np.float32)[None])
-    sine = jnp.asarray(np.sin(angle).astype(np.float32)[None])
+    circle = jnp.asarray(np.stack([np.cos(angle), np.sin(angle)]).astype(np.float32))
     vmem = pl.BlockSpec(memory_space=pltpu.VMEM)
-    smem = pl.BlockSpec(memory_space=pltpu.SMEM)
+    hbm = pl.BlockSpec(memory_space=pltpu.HBM)
     dma = pltpu.SemaphoreType.DMA
     blocks = (z.chips, z.chunks, z.block, LANES)
     flops = 4 * z.rows * z.feat * LANES
-    bp, cw, ln = pl.pallas_call(
+    sums, ln_row = pl.pallas_call(
         functools.partial(kernel, z),
         out_shape=(
-            jax.ShapeDtypeStruct((1, z.orient, z.feat), F32),
-            jax.ShapeDtypeStruct((1, z.orient), F32),
-            jax.ShapeDtypeStruct((1, z.parts), F32),
+            jax.ShapeDtypeStruct((z.chunks * z.block, LANES), F32),
+            jax.ShapeDtypeStruct((1, LANES), F32),
         ),
-        in_specs=[pl.BlockSpec(memory_space=pl.ANY), vmem, vmem, vmem, smem, smem, vmem, vmem],
-        out_specs=(vmem, vmem, vmem),
+        in_specs=[hbm] * 7,
+        out_specs=(vmem, vmem),
         scratch_shapes=[
+            pltpu.VMEM((1, z.orient, z.feat), BF16),
+            pltpu.VMEM((z.tiles, LANES), F32),
+            pltpu.VMEM((2, LANES), jnp.int32),
+            pltpu.SMEM((z.parts,), jnp.int32),
+            pltpu.SMEM((z.parts,), jnp.int32),
+            pltpu.VMEM((2, LANES), F32),
             pltpu.VMEM((2, z.parts, z.feat), BF16),
             pltpu.VMEM((2 * z.tiles * z.imgs, LANES), F32),
             pltpu.VMEM((z.tiles, LANES, 2 * LANES), BF16),
@@ -546,8 +599,8 @@
             pltpu.VMEM(blocks, BF16),
             pltpu.VMEM(blocks, BF16),
             pltpu.VMEM((z.chunks, z.block, LANES), F32),
-            pltpu.VMEM((z.chunks * z.block, LANES), F32),
             dma,
+            dma((6,)),
             dma((2,)),
             dma((2,)),
             dma((z.chips, z.chunks)),
@@ -558,7 +611,7 @@
             dma((z.chips, z.chunks)),
         ],
         compiler_params=pltpu.CompilerParams(
-            collective_id=0, has_side_effects=True, vmem_limit_bytes=40 * 2**20
+            collective_id=0, has_side_effects=True, vmem_limit_bytes=65536 * 2**10
         ),
         cost_estimate=pl.CostEstimate(
             flops=flops, bytes_accessed=4 * 2**20, transcendentals=z.rows * LANES
@@ -567,12 +620,27 @@
         particles,
         references,
         inv_noise.reshape(z.tiles, LANES),
-        shifts,
+        shifts.T,
         prior_class,
         prior_orient,
-        cosine,
-        sine,
+        circle,
     )
+    bp, cw, ln = pl.pallas_call(
+        functools.partial(finish, z),
+        out_shape=(
+            jax.ShapeDtypeStruct((1, z.orient, z.feat), F32),
+            jax.ShapeDtypeStruct((1, z.orient), F32),
+            jax.ShapeDtypeStruct((1, z.parts), F32),
+        ),
+        in_specs=[vmem, vmem],
+        out_specs=(hbm, hbm, hbm),
+        scratch_shapes=[
+            pltpu.VMEM((1, z.orient, z.feat), F32),
+            pltpu.VMEM((1, z.orient), F32),
+            pltpu.VMEM((1, z.parts), F32),
+            dma((3,)),
+        ],
+    )(sums, ln_row)
     return bp, cw, ln.reshape(z.parts)
 
 

time: 42.3 us -> 38.9 us (0.920)
  local copies, waits for them, and re-layouts: 5 us -> 0 us
  Pallas kernels: 36.3 us -> 38.1 us
    unnamed x18 -> x0, local copies, waits for them, and re-layouts: 5 us -> none
    pallas_call x0 -> x1, Pallas kernels: none -> 1.67 us  [on_device(): pl.pallas_call(functools.partial(finish, z), out_shape=(jax.ShapeDtypeStr...]
where the time goes in v3:
time: 38.9 us; the launch traced here: 38.8 us
  Pallas kernels  38.1 us (98%)
  between operations  0.64 us (2%)
    pallas_call x1, Pallas kernels, on_device(): pl.pallas_call(functools.partial(kernel, z), out_shape=(jax.ShapeDtypeStr...  36.5 us
    pallas_call x1, Pallas kernels, on_device(): pl.pallas_call(functools.partial(finish, z), out_shape=(jax.ShapeDtypeStr...  1.67 us

profile of v3, /device:TPU:1, one launch (start us, length us, event | category | flops | bytes accessed | tf_op | source)
XLA Modules:
  0.0 38.8 jit_solution(2209091138879435239)
XLA Ops:
  0.6 36.5 %shard_map.94 = (f32[280,128]{1,0:T(8,128)}, f32[1,128]{1,0:T(1,128)}) custom-call(bf16[16,16640]{1,0:T(8,128)(2,1)} %x_hbm.1, bf16[1,2,16640]{2,1,0:T(2,128)(2,1)} %ref_hbm.1, f32[65,128]{1,0:T(8,128)} %bitcast.3, s32[2,128]{1,0:T(2,128)} %bitcast.4, s32[16]{0:T(128)} %pc_hbm.1, s32[16]{0:T(128)} %po_hbm.1, f32[2,128]{1,0:T(2,128)} %constant.2.clone.circle_hbm), custom_call_target="tpu_custom_call" | custom-call | flops 4362076160 | bytes 4194304 | tf_op jit(solution)/shard_map/pallas_call | solution.py:567
  37.1 1.7 %shard_map.95 = (f32[1,2,16640]{2,1,0:T(2,128)}, f32[1,2]{1,0:T(1,128)}, f32[1,16]{1,0:T(1,128)}) custom-call(f32[280,128]{1,0:T(8,128)} %get-tuple-element.8.sum_ref, f32[1,128]{1,0:T(1,128)} %get-tuple-element.9.ln_ref), custom_call_target="tpu_custom_call" | custom-call | tf_op jit(solution)/shard_map/pallas_call | solution.py:628

commit v4 on v3

v4 whole, which is shorter than its diff:
```python
import functools
import math

import jax
import jax.numpy as jnp
import numpy as np
from jax import lax
from jax.experimental import pallas as pl
from jax.experimental.pallas import tpu as pltpu
from jax.sharding import PartitionSpec as P

L = 128
LANES = 128
PRIOR_LOG_BOOST = 12.0
MESH = pl.DeviceIdType.MESH
F32 = jnp.float32
BF16 = jnp.bfloat16


class Run:
    def __init__(self, n, first, count, half, orient):
        self.n = n
        self.first = first
        self.count = count
        self.half = half
        self.stride = 2 * half
        self.block = orient * self.stride


class Sizes:
    def __init__(self, n_dom, n_cls, parts, orient, feat):
        self.chips = n_dom // 2
        self.n_cls = n_cls
        self.parts = parts
        self.orient = orient
        self.orient_all = orient * n_cls
        self.feat = feat
        self.tiles = feat // 2 // LANES
        n = 14
        count = self.tiles // n
        left = self.tiles - n * count
        self.lead = Run(left, 0, 1, left + 1, orient)
        self.bulk = Run(n, left, count, n, orient)
        self.runs = (self.lead, self.bulk)
        self.refs = self.chips * orient
        self.imgs = 2 * parts
        self.rows = self.imgs * self.refs
        self.group = 2 * n_cls


class Bufs:
    def __init__(
        self,
        run,
        rows,
        send,
        recv,
        wide,
        back,
        back_send,
        back_recv,
        back_own,
        ssem,
        rsem,
        back_ssem,
        back_rsem,
    ):
        self.run = run
        self.rows = rows
        self.send = send
        self.recv = recv
        self.wide = wide
        self.back = back
        self.back_send = back_send
        self.back_recv = back_recv
        self.back_own = back_own
        self.ssem = ssem
        self.rsem = rsem
        self.back_ssem = back_ssem
        self.back_rsem = back_rsem


def place(z, tile):
    part, kt = divmod(tile, z.tiles)
    if kt < z.lead.n:
        return 0, 0, part * z.lead.half + kt
    s, k = divmod(kt - z.lead.n, z.bulk.n)
    return 1, s, part * z.bulk.half + k


def kernel(
    z,
    x_hbm,
    ref_hbm,
    w_hbm,
    shift_hbm,
    pc_hbm,
    po_hbm,
    circle_hbm,
    bp_ref,
    cw_ref,
    ln_ref,
    ref_ref,
    w_ref,
    shift_ref,
    pc_ref,
    po_ref,
    circle_ref,
    xb,
    x32,
    tab,
    prior,
    acc,
    power,
    top,
    total,
    stats,
    scale,
    post,
    weight,
    x_sem,
    in_sem,
    pair_send,
    pair_recv,
    stat_ssem,
    stat_rsem,
    *per_run,
):
    size = len(per_run) // 2
    runs = [Bufs(r, *per_run[n * size : (n + 1) * size]) for n, r in enumerate(z.runs)]
    lead, bulk = runs
    dom = lax.axis_index("dom")
    cls = lax.axis_index("cls")
    chip = dom // 2
    core = lax.rem(dom, 2)
    slot = cls * 2 + core
    other = 1 - core

    own_x = pltpu.make_async_copy(x_hbm, xb.at[core], x_sem)
    small = [
        pltpu.make_async_copy(src, dst, in_sem.at[n])
        for n, (src, dst) in enumerate(
            (
                (ref_hbm, ref_ref),
                (pc_hbm, pc_ref),
                (po_hbm, po_ref),
                (shift_hbm, shift_ref),
                (circle_hbm, circle_ref),
                (w_hbm, w_ref),
            )
        )
    ]
    def wait_all(like, sem):
        pltpu.make_async_copy(like, like, sem).wait()

    def same_core(step):
        peer_chip = lax.rem(chip + step, z.chips)
        return peer_chip, (peer_chip * 2 + core, cls)

    def same_images(step):
        peer = lax.rem(slot + step, z.group)
        return peer, (chip * 2 + lax.rem(peer, 2), peer // 2)

    barrier = pltpu.get_barrier_semaphore()

    def greet_refs(step, c):
        _, device = same_core(step)
        pl.semaphore_signal(barrier, inc=1, device_id=device, device_id_type=MESH)
        return c

    def greet_stats(step, c):
        _, device = same_images(step)
        pl.semaphore_signal(barrier, inc=1, device_id=device, device_id_type=MESH)
        return c

    lax.fori_loop(1, z.chips, greet_refs, 0)
    lax.fori_loop(1, z.group, greet_stats, 0)

    for copy in small:
        copy.start()
    own_x.start()

    for copy in small:
        copy.wait()

    for tile in range(2 * z.tiles):
        n, s, row = place(z, tile)
        start = s * z.runs[n].block + row
        runs[n].rows[pl.ds(start, z.orient, stride=z.runs[n].stride), :] = ref_ref[
            0, :, tile * LANES : (tile + 1) * LANES
        ].astype(F32)
    for b in runs:
        for s in range(b.run.count):
            rows = b.rows[s * b.run.block : (s + 1) * b.run.block, :].astype(BF16)
            b.send[s] = rows
            b.recv[chip, s] = rows
    pl.semaphore_wait(barrier, z.chips - 1 + z.group - 1)

    def pair_copies():
        device = (chip * 2 + other, cls)
        return (
            pltpu.make_async_remote_copy(
                src_ref=x_hbm,
                dst_ref=xb.at[core],
                send_sem=pair_send.at[0],
                recv_sem=pair_recv.at[0],
                device_id=device,
                device_id_type=MESH,
            ),
            pltpu.make_async_remote_copy(
                src_ref=prior.at[core],
                dst_ref=prior.at[core],
                send_sem=pair_send.at[1],
                recv_sem=pair_recv.at[1],
                device_id=device,
                device_id_type=MESH,
            ),
        )

    pair = pair_copies()
    def ref_copy(b, s, step):
        _, device = same_core(step)
        return pltpu.make_async_remote_copy(
            src_ref=b.send.at[s],
            dst_ref=b.recv.at[chip, s],
            send_sem=b.ssem,
            recv_sem=b.rsem.at[s],
            device_id=device,
            device_id_type=MESH,
        )

    for b in runs:

        def send_refs(s, c, b=b):
            def to_peer(step, c):
                ref_copy(b, s, step).start()
                return c

            return lax.fori_loop(1, z.chips, to_peer, c)

        lax.fori_loop(0, b.run.count, send_refs, 0)
        if b is lead:
            pair[0].start()

    for i in range(z.parts):
        value = (pc_ref[i] * z.orient_all + po_ref[i]).astype(F32)
        prior[core, i : i + 1, :] = jnp.full((1, LANES), value, F32)
    pair[1].start()

    lane = lax.broadcasted_iota(jnp.int32, (1, LANES), 1)
    half_width = L // 2 + 1

    def look_up(turn):
        turn = turn.astype(jnp.int32) & (L - 1)
        return tuple(
            jnp.take_along_axis(
                jnp.broadcast_to(ref[...], (8, LANES)), turn, axis=1, mode="promise_in_bounds"
            )
            for ref in (circle_ref.at[0:1], circle_ref.at[1:2])
        )

    lane8 = lax.broadcasted_iota(jnp.int32, (8, LANES), 1)
    sub8 = lax.broadcasted_iota(jnp.int32, (8, LANES), 0)
    shift_rows = shift_ref[...].astype(F32)
    first_row = jnp.where(lane8 >= half_width, 1, 0)
    first_col = lane8 - half_width * first_row
    rows_on, rows_over = divmod(LANES, half_width)
    rows_on, rows_back = rows_on + 1, half_width - rows_over
    span = 8
    unroll = 13 if z.tiles % 13 == 0 else 1
    for t0 in range(0, LANES, 8 * span):
        start, turns = [], []
        for v in range(span):
            rows = slice(t0 + 8 * v, t0 + 8 * v + 8)
            here = lane8 - sub8 == rows.start
            shift_x, shift_y = (
                jnp.broadcast_to(
                    jnp.sum(
                        jnp.where(here, jnp.broadcast_to(shift_rows[n : n + 1, :], (8, LANES)), 0.0),
                        axis=1,
                        keepdims=True,
                    ),
                    (8, LANES),
                )
                for n in range(2)
            )
            start.append(
                look_up(first_col.astype(F32) * shift_x + first_row.astype(F32) * shift_y)
            )
            turns.append(
                (
                    look_up(rows_on * shift_y - rows_back * shift_x),
                    look_up((rows_on - 1) * shift_y + rows_over * shift_x),
                )
            )

        def make_table(step, carry):
            now, col = carry
            for j in range(unroll):
                kt = step * unroll + j
                near = col >= rows_back
                col = jnp.where(near, col - rows_back, col + rows_over)
                after = []
                for v in range(span):
                    cosine, sine = now[v]
                    rows = slice(t0 + 8 * v, t0 + 8 * v + 8)
                    tab[kt, rows, :LANES] = cosine.astype(BF16)
                    tab[kt, rows, LANES:] = sine.astype(BF16)
                    turn_cos = jnp.where(near, turns[v][0][0], turns[v][1][0])
                    turn_sin = jnp.where(near, turns[v][0][1], turns[v][1][1])
                    after.append(
                        (
                            cosine * turn_cos - sine * turn_sin,
                            sine * turn_cos + cosine * turn_sin,
                        )
                    )
                now = tuple(after)
            return now, col

        lax.fori_loop(0, z.tiles // unroll, make_table, (tuple(start), first_col))

    own_x.wait()
    for copy in pair:
        copy.wait_recv()

    def widen(tile, c):
        at = pl.multiple_of(tile * LANES, LANES)
        to = pl.multiple_of(tile * z.imgs, 8)
        for half in range(2):
            x32[pl.ds(to + half * z.parts, z.parts), :] = xb[half, :, pl.ds(at, LANES)].astype(F32)
        return c

    lax.fori_loop(0, 2 * z.tiles, widen, 0)

    def image_row(tile, i):
        return x32[pl.ds(tile * z.imgs + i, 8, stride=0), :]

    halves = z.refs // 8
    acc[...] = jnp.zeros_like(acc)
    power[...] = jnp.zeros_like(power)

    def score_chunk(b, s):
        run = b.run

        wait_all(b.recv.at[pl.ds(0, z.chips - 1), s], b.rsem.at[s])
        for peer in range(z.chips):
            b.wide[peer * run.block : (peer + 1) * run.block, :] = b.recv[peer, s].astype(F32)

        def tile_step(k):
            kt = run.first + s * run.n + k
            noise = w_ref[pl.ds(kt, 8, stride=0), :]
            real, imag = [], []
            for h in range(halves):
                first = h * 8 * run.stride + k
                a_real = b.wide[pl.ds(first, 8, stride=run.stride), :]
                a_imag = b.wide[pl.ds(first + run.half, 8, stride=run.stride), :]
                w_real = noise * a_real
                w_imag = noise * a_imag
                power[h * 8 : (h + 1) * 8, :] += w_real * a_real + w_imag * a_imag
                real.append(w_real)
                imag.append(w_imag)
            lhs = []
            for i in range(z.imgs):
                x_real = image_row(kt, i)
                x_imag = image_row(z.tiles + kt, i)
                p_real = jnp.concatenate(
                    [real[h] * x_real + imag[h] * x_imag for h in range(halves)], 0
                )
                p_imag = jnp.concatenate(
                    [real[h] * x_imag - imag[h] * x_real for h in range(halves)], 0
                )
                lhs.append(jnp.concatenate([p_real.astype(BF16), p_imag.astype(BF16)], 1))
            acc[...] += lax.dot_general(
                jnp.concatenate(lhs, 0),
                tab[kt],
                (((1,), (1,)), ((), ())),
                preferred_element_type=F32,
            )

        for k in range(run.n):
            tile_step(k)

    def score_bulk(s, c):
        score_chunk(bulk, s)
        return c

    score_chunk(lead, 0)
    lax.fori_loop(0, bulk.run.count, score_bulk, 0)

    row = lax.broadcasted_iota(jnp.int32, (z.refs, LANES), 0)
    class_id = 2 * (row // z.orient) + core
    ref_id = class_id * z.orient_all + cls * z.orient + lax.rem(row, z.orient)
    ref_id = ref_id.astype(F32)
    half_power = 0.5 * jnp.sum(power[...], axis=1, keepdims=True)
    for i in range(z.imgs):
        half, il = divmod(i, z.parts)
        block = acc[i * z.refs : (i + 1) * z.refs, :] - half_power
        block = block + jnp.where(prior[half, il : il + 1, :] == ref_id, PRIOR_LOG_BOOST, 0.0)
        acc[i * z.refs : (i + 1) * z.refs, :] = block
        top[i : i + 1, :] = jnp.max(block, axis=0, keepdims=True)
    top[...] = jnp.broadcast_to(jnp.max(top[...], axis=1, keepdims=True), top.shape)
    for i in range(z.imgs):
        block = jnp.exp(acc[i * z.refs : (i + 1) * z.refs, :] - top[i : i + 1, :])
        acc[i * z.refs : (i + 1) * z.refs, :] = block
        total[i : i + 1, :] = jnp.sum(block, axis=0, keepdims=True)
    sums = jnp.sum(total[...], axis=1, keepdims=True)
    groups = z.imgs // 8
    packed = jnp.zeros((8, LANES), F32)
    for v in range(groups):
        packed = jnp.where(lane8 == v, top[v * 8 : (v + 1) * 8, :], packed)
        packed = jnp.where(lane8 == groups + v, sums[v * 8 : (v + 1) * 8, :], packed)
    stats[slot] = packed

    def stat_copy(step):
        _, device = same_images(step)
        return pltpu.make_async_remote_copy(
            src_ref=stats.at[slot],
            dst_ref=stats.at[slot],
            send_sem=stat_ssem,
            recv_sem=stat_rsem,
            device_id=device,
            device_id_type=MESH,
        )

    def send_stat(step, c):
        stat_copy(step).start()
        return c

    lax.fori_loop(1, z.group, send_stat, 0)
    wait_all(stats.at[pl.ds(0, z.group - 1)], stat_rsem)

    all_top = stats[0]
    for g in range(1, z.group):
        all_top = jnp.maximum(all_top, stats[g])
    all_total = jnp.zeros((8, LANES), F32)
    for g in range(z.group):
        part = stats[g]
        all_total = all_total + jnp.exp(part - all_top) * pltpu.roll(part, LANES - groups, 1)
    log_norm = all_top + jnp.log(all_total)
    rescale = jnp.exp(packed - log_norm)
    for v in range(groups):
        scale[v * 8 : (v + 1) * 8, :] = jnp.broadcast_to(rescale[:, v : v + 1], (8, LANES))
        total[v * 8 : (v + 1) * 8, :] = jnp.broadcast_to(log_norm[:, v : v + 1], (8, LANES))
    mass = jnp.zeros((z.refs, LANES), F32)
    for i in range(z.imgs):
        block = acc[i * z.refs : (i + 1) * z.refs, :] * scale[i : i + 1, :]
        mass = mass + block
        post[i * z.refs : (i + 1) * z.refs, :] = block.astype(BF16)
    weight[...] = jnp.broadcast_to(jnp.sum(mass, axis=1, keepdims=True), weight.shape)

    def back_copy(b, s, step):
        peer, device = same_core(step)
        return pltpu.make_async_remote_copy(
            src_ref=b.back_send.at[peer, s],
            dst_ref=b.back_recv.at[chip, s],
            send_sem=b.back_ssem,
            recv_sem=b.back_rsem.at[s],
            device_id=device,
            device_id_type=MESH,
        )

    def back_chunk(b, s):
        run = b.run

        def tile_step(k):
            kt = run.first + s * run.n + k
            coeff = jnp.dot(post[...], tab[kt], preferred_element_type=F32)
            real = [jnp.zeros((8, LANES), F32) for _ in range(halves)]
            imag = [jnp.zeros((8, LANES), F32) for _ in range(halves)]
            for i in range(z.imgs):
                x_real = image_row(kt, i)
                x_imag = image_row(z.tiles + kt, i)
                for h in range(halves):
                    at = i * z.refs + h * 8
                    cosine = coeff[at : at + 8, :LANES]
                    sine = coeff[at : at + 8, LANES:]
                    real[h] = real[h] + (x_real * cosine + x_imag * sine)
                    imag[h] = imag[h] + (x_imag * cosine - x_real * sine)
            for h in range(halves):
                first = h * 8 * run.stride + k
                b.back[pl.ds(first, 8, stride=run.stride), :] = real[h]
                b.back[pl.ds(first + run.half, 8, stride=run.stride), :] = imag[h]

        for k in range(run.n):
            tile_step(k)
        if run.half > run.n:
            high = weight[...].astype(BF16).astype(F32)
            low = weight[...] - high
            for h in range(halves):
                first = h * 8 * run.stride + run.n
                rows = slice(h * 8, (h + 1) * 8)
                b.back[pl.ds(first, 8, stride=run.stride), :] = high[rows]
                b.back[pl.ds(first + run.half, 8, stride=run.stride), :] = low[rows]
        for peer in range(z.chips):
            b.back_send[peer, s] = b.back[peer * run.block : (peer + 1) * run.block, :].astype(BF16)
        b.back_own[s] = b.back[pl.ds(pl.multiple_of(chip * run.block, 8), run.block), :]

        def to_peer(step, c):
            back_copy(b, s, step).start()
            return c

        lax.fori_loop(1, z.chips, to_peer, 0)

    def back_bulk(s, c):
        back_chunk(bulk, s)
        return c

    lax.fori_loop(0, bulk.run.count, back_bulk, 0)
    back_chunk(lead, 0)

    for copy in pair:
        copy.wait_send()

    for b in runs:
        wait_all(b.recv.at[pl.ds(0, z.chips - 1)], b.ssem)
        wait_all(b.back_recv.at[pl.ds(0, z.chips - 1)], b.back_ssem)
    wait_all(stats.at[pl.ds(0, z.group - 1)], stat_ssem)

    mine = total[pl.ds(pl.multiple_of(core * z.parts, 8), z.parts), :]
    diagonal = lax.broadcasted_iota(jnp.int32, (z.parts, LANES), 0) == lax.broadcasted_iota(
        jnp.int32, (z.parts, LANES), 1
    )
    ln_ref[...] = jnp.sum(jnp.where(diagonal, mine, 0.0), axis=0, keepdims=True)[:, : z.parts]

    for b in (bulk, lead):
        run = b.run

        def gather_chunk(s, c, b=b):
            wait_all(b.back_recv.at[pl.ds(0, z.chips - 1), s], b.back_rsem.at[s])

            def add(step, got):
                peer, _ = same_core(step)
                return got + b.back_recv[peer, s].astype(F32)

            at = pl.multiple_of(s * b.run.block, 8)
            b.rows[pl.ds(at, b.run.block), :] = lax.fori_loop(1, z.chips, add, b.back_own[s])
            return c

        lax.fori_loop(0, run.count, gather_chunk, 0)
        for tile in range(2 * z.tiles):
            n, s, row = place(z, tile)
            if runs[n] is b:
                bp_ref[0, :, tile * LANES : (tile + 1) * LANES] = b.rows[
                    pl.ds(s * run.block + row, z.orient, stride=run.stride), :
                ]
    line = jnp.zeros((1, LANES), F32)
    for o in range(z.orient):
        at = o * lead.run.stride + lead.run.n
        low = at + lead.run.half
        line = jnp.where(lane == o, lead.rows[at : at + 1, :] + lead.rows[low : low + 1, :], line)
    cw_ref[...] = line[:, : z.orient]


def finish(bp_in, cw_in, ln_in, bp_ref, cw_ref, ln_ref, sem):
    copies = [
        pltpu.make_async_copy(src, dst, sem.at[n])
        for n, (src, dst) in enumerate(((bp_in, bp_ref), (cw_in, cw_ref), (ln_in, ln_ref)))
    ]
    for copy in copies:
        copy.start()
    for copy in copies:
        copy.wait()


def on_device(z, particles, references, inv_noise, shifts, prior_class, prior_orient):
    angle = (np.arange(L, dtype=np.float32) * np.float32(2.0 * math.pi / L)).astype(np.float64)
    circle = jnp.asarray(np.stack([np.cos(angle), np.sin(angle)]).astype(np.float32))
    vmem = pl.BlockSpec(memory_space=pltpu.VMEM)
    hbm = pl.BlockSpec(memory_space=pltpu.HBM)
    dma = pltpu.SemaphoreType.DMA
    flops = 4 * z.rows * z.feat * LANES
    per_run = []
    for run in z.runs:
        per_run += [
            pltpu.VMEM((run.count * run.block, LANES), F32),
            pltpu.VMEM((run.count, run.block, LANES), BF16),
            pltpu.VMEM((z.chips, run.count, run.block, LANES), BF16),
            pltpu.VMEM((z.chips * run.block, LANES), F32),
            pltpu.VMEM((z.chips * run.block, LANES), F32),
            pltpu.VMEM((z.chips, run.count, run.block, LANES), BF16),
            pltpu.VMEM((z.chips, run.count, run.block, LANES), BF16),
            pltpu.VMEM((run.count, run.block, LANES), F32),
            dma,
            dma((run.count,)),
            dma,
            dma((run.count,)),
        ]
    outs = (
        jax.ShapeDtypeStruct((1, z.orient, z.feat), F32),
        jax.ShapeDtypeStruct((1, z.orient), F32),
        jax.ShapeDtypeStruct((1, z.parts), F32),
    )
    parts = pl.pallas_call(
        functools.partial(kernel, z),
        out_shape=outs,
        in_specs=[hbm] * 7,
        out_specs=(vmem, vmem, vmem),
        scratch_shapes=[
            pltpu.VMEM((1, z.orient, z.feat), BF16),
            pltpu.VMEM((z.tiles, LANES), F32),
            pltpu.VMEM((2, LANES), jnp.int32),
            pltpu.SMEM((z.parts,), jnp.int32),
            pltpu.SMEM((z.parts,), jnp.int32),
            pltpu.VMEM((2, LANES), F32),
            pltpu.VMEM((2, z.parts, z.feat), BF16),
            pltpu.VMEM((2 * z.tiles * z.imgs, LANES), F32),
            pltpu.VMEM((z.tiles, LANES, 2 * LANES), BF16),
            pltpu.VMEM((2, z.parts, LANES), F32),
            pltpu.VMEM((z.rows, LANES), F32),
            pltpu.VMEM((z.refs, LANES), F32),
            pltpu.VMEM((z.imgs, LANES), F32),
            pltpu.VMEM((z.imgs, LANES), F32),
            pltpu.VMEM((z.group, 8, LANES), F32),
            pltpu.VMEM((z.imgs, LANES), F32),
            pltpu.VMEM((z.rows, LANES), BF16),
            pltpu.VMEM((z.refs, LANES), F32),
            dma,
            dma((6,)),
            dma((2,)),
            dma((2,)),
            dma,
            dma,
            *per_run,
        ],
        compiler_params=pltpu.CompilerParams(
            collective_id=0, has_side_effects=True, vmem_limit_bytes=64 * 2**20
        ),
        cost_estimate=pl.CostEstimate(
            flops=flops, bytes_accessed=4 * 2**20, transcendentals=z.rows * LANES
        ),
    )(
        particles,
        references,
        inv_noise.reshape(z.tiles, LANES),
        shifts.T,
        prior_class,
        prior_orient,
        circle,
    )
    bp, cw, ln = pl.pallas_call(
        finish,
        out_shape=outs,
        in_specs=[vmem] * 3,
        out_specs=(hbm,) * 3,
        scratch_shapes=[dma((3,))],
    )(*parts)
    return bp, cw, ln.reshape(z.parts)


def solution(mesh):
    def body(particles, references, inv_noise, shifts, prior_class, prior_orient):
        n_dom, n_cls = lax.axis_size("dom"), lax.axis_size("cls")
        z = Sizes(n_dom, n_cls, particles.shape[0], references.shape[1], particles.shape[1])
        return on_device(z, particles, references, inv_noise, shifts, prior_class, prior_orient)

    placed = (P("dom", None), P("dom", "cls", None), P(), P(), P("dom"), P("dom"))
    return jax.shard_map(
        body,
        mesh=mesh,
        in_specs=placed,
        out_specs=(P("dom", "cls", None), P("dom", "cls"), P("dom")),
        check_vma=False,
    )
```

time: 38.9 us -> 36.3 us (0.933)
  Pallas kernels: 38.1 us -> 35.5 us
    pallas_call x2, Pallas kernels: 38.1 us -> 35.5 us  [the longest x1 33.9 us: on_device(): pl.pallas_call(functools.partial(kernel, z), out_shape=outs, in_specs=[hb...]
where the time goes in v4:
time: 36.3 us; the launch traced here: 36.2 us
  Pallas kernels  35.5 us (98%)
  between operations  0.64 us (2%)
    pallas_call x1, Pallas kernels, on_device(): pl.pallas_call(functools.partial(kernel, z), out_shape=outs, in_specs=[hb...  33.9 us
    pallas_call x1, Pallas kernels, on_device(): pl.pallas_call(finish, out_shape=outs, in_specs=[vmem] * 3, out_specs=(hb...  1.6 us

profile of v4, /device:TPU:1, one launch (start us, length us, event | category | flops | bytes accessed | tf_op | source)
XLA Modules:
  0.0 36.2 jit_solution(11538216016184257659)
XLA Ops:
  0.6 33.9 %shard_map.94 = (f32[1,2,16640]{2,1,0:T(2,128)}, f32[1,2]{1,0:T(1,128)}, f32[1,16]{1,0:T(1,128)}) custom-call(bf16[16,16640]{1,0:T(8,128)(2,1)} %x_hbm.1, bf16[1,2,16640]{2,1,0:T(2,128)(2,1)} %ref_hbm.1, f32[65,128]{1,0:T(8,128)} %bitcast.3, s32[2,128]{1,0:T(2,128)} %bitcast.4, s32[16]{0:T(128)} %pc_hbm.1, s32[16]{0:T(128)} %po_hbm.1, ...), custom_call_target="tpu_custom_call" | custom-call | flops 4362076160 | bytes 4194304 | tf_op jit(solution)/shard_map/pallas_call | solution.py:593
  34.6 1.6 %shard_map.95 = (f32[1,2,16640]{2,1,0:T(2,128)}, f32[1,2]{1,0:T(1,128)}, f32[1,16]{1,0:T(1,128)}) custom-call(f32[1,2,16640]{2,1,0:T(2,128)} %get-tuple-element.9.bp_in, f32[1,2]{1,0:T(1,128)} %get-tuple-element.10.cw_in, f32[1,16]{1,0:T(1,128)} %get-tuple-element.11.ln_in), custom_call_target="tpu_custom_call" | custom-call | tf_op jit(solution)/shard_map/pallas_call | solution.py:640
